TPU v7x, 128 devices: a whole 4x4x4 slice. The times are simulated.
128 devices in a mesh: pair: 8 (over z, core), tm: 16 (over y, x).
Axes of the slice: x: 4, y: 4, z: 4, core: 2. Of those that a mesh axis runs over, the one named last changes fastest.
Arguments:
- records: bfloat16 [512, 256, 2048], P('pair', 'tm'), may hold values from -60 to 60, as said below
- pair_list: int32 [1024, 2], replicated, may hold values from 0 to 511, as said below
- sketch: float32 [16, 2048], replicated, may hold values from -6 to 6
Outputs:
- stacks: float32 [1024, 2048], P('pair')
Inputs may be any that keep to these rules, and one draw needn't show every extreme that they name: `pair_list`: rows p * 128 to (p + 1) * 128 - 1 name at most 12 distinct channels from any one block of channels o * 64 to (o + 1) * 64 - 1, and exactly 12 from one such block; the 256 channel slots of a pair index cycle through its listed channels, so each listed channel is used. `records`: each channel is a delayed copy of a field common to all channels plus its own noise, times a channel gain.
All inputs are finite; a program needn't handle non-finite values.
Results may differ from a plain program's by a relative error of at most 0.0041.
The roundings to bfloat16 on the way count: a program that leaves them out, or rounds other values in their place, can miss the bound.
Values may be sent and summed in bfloat16 or wider, within the bound.
No kernel may reach another device: no remote copies, remote signals or barrier semaphores. Data moves between devices by JAX's collectives and lax.ppermute only.
A program may use at most 192 MiB of HBM per device.

v0:
```python
import math

import jax
import jax.numpy as jnp
from jax import lax
from jax.sharding import PartitionSpec as P

SAMPLES = 2048
NF = 512
LAGS = 2048
CAP = 12
PAIRS_DEV = 128


def tables():
    freq = NF // 2 + jnp.arange(NF)
    times = jnp.arange(SAMPLES)
    turn = jnp.mod(times[:, None] * freq[None, :], SAMPLES).astype(jnp.float32) * (
        2.0 * math.pi / SAMPLES
    )
    forward = jnp.concatenate([jnp.cos(turn), jnp.sin(turn)], axis=1).astype(jnp.bfloat16)
    shifts = jnp.arange(LAGS) - LAGS // 2
    angle = jnp.mod(freq[:, None] * shifts[None, :], SAMPLES).astype(jnp.float32) * (
        2.0 * math.pi / SAMPLES
    )
    inverse = (jnp.concatenate([jnp.cos(angle), -jnp.sin(angle)], axis=0) / math.sqrt(NF)).astype(
        jnp.bfloat16
    )
    return (forward, inverse)


def whiten(block, forward):
    spectra = jnp.dot(block, forward, preferred_element_type=jnp.float32)
    real_part = spectra[:, :NF]
    imag_part = spectra[:, NF:]
    power = real_part * real_part + imag_part * imag_part
    level = jnp.mean(power, axis=1, keepdims=True)
    factor = lax.rsqrt(power + level + 1e-06)
    return jnp.concatenate([real_part * factor, imag_part * factor], axis=1).astype(jnp.bfloat16)


def correlate(first, second):
    left = first.astype(jnp.float32)
    right = second.astype(jnp.float32)
    lre, lim = (left[..., :NF], left[..., NF:])
    rre, rim = (right[..., :NF], right[..., NF:])
    return jnp.concatenate([lre * rre + lim * rim, lim * rre - lre * rim], axis=-1).astype(
        jnp.bfloat16
    )


def orthonormal(raw):
    highest = lax.Precision.HIGHEST
    gram = jnp.einsum("prl,psl->prs", raw, raw, precision=highest)
    lower = jnp.linalg.cholesky(gram)
    return lax.linalg.triangular_solve(lower, raw, left_side=True, lower=True)


def local(records, pair_list, sketch):
    highest = lax.Precision.HIGHEST
    forward, inverse = tables()
    n_pair = lax.axis_size("pair")
    owner = lax.axis_index("pair")
    ch_dev, win_dev, samples = records.shape
    white = whiten(records.reshape(ch_dev * win_dev, samples), forward).reshape(
        ch_dev, win_dev, 2 * NF
    )
    mine = lax.dynamic_slice_in_dim(pair_list, owner * PAIRS_DEV, PAIRS_DEV, 0)
    wanted = pair_list.reshape(n_pair, 2 * PAIRS_DEV) - owner * ch_dev
    column = jnp.arange(ch_dev)
    asked = jnp.any(wanted[:, None, :] == column[None, :, None], axis=2)
    order = jnp.cumsum(asked.astype(jnp.int32), axis=1) - 1
    slots = jnp.arange(CAP)
    picker = (asked[:, None, :] & (order[:, None, :] == slots[None, :, None])).astype(jnp.bfloat16)
    outgoing = jnp.einsum(
        "dkc,cwf->dkwf", picker, white, preferred_element_type=jnp.float32
    ).astype(jnp.bfloat16)
    everyone = jnp.arange(n_pair * ch_dev)
    held = jnp.any(mine.reshape(-1)[None, :] == everyone[:, None], axis=1).reshape(n_pair, ch_dev)
    rank_of = (jnp.cumsum(held.astype(jnp.int32), axis=1) - 1).reshape(-1)
    first_slot = mine[:, 0] // ch_dev * CAP + jnp.take(rank_of, mine[:, 0])
    second_slot = mine[:, 1] // ch_dev * CAP + jnp.take(rank_of, mine[:, 1])
    arrived = lax.all_to_all(outgoing, "pair", split_axis=0, concat_axis=0, tiled=True)
    flat = arrived.reshape(n_pair * CAP, arrived.shape[2], arrived.shape[3])
    cross = correlate(jnp.take(flat, first_slot, axis=0), jnp.take(flat, second_slot, axis=0))
    crossf = cross.astype(jnp.float32)
    energy_local = jnp.sum(crossf * crossf, axis=(1, 2))
    lagged = jnp.einsum("pwf,fl->pwl", cross, inverse, preferred_element_type=jnp.float32)
    probe = jnp.einsum("pwl,rl->pwr", lagged, sketch, precision=highest)
    partial_raw = jnp.einsum("pwr,pwl->prl", probe, lagged, precision=highest)
    raw, energy = lax.psum((partial_raw, energy_local), "tm")
    basis = orthonormal(raw)
    coeffs = jnp.einsum("pwl,prl->pwr", lagged, basis, precision=highest)
    total, power = lax.psum((jnp.sum(coeffs, axis=1), jnp.sum(coeffs * coeffs, axis=1)), "tm")
    gain = power / (power + energy[:, None] / (2 * NF))
    windows = win_dev * lax.axis_size("tm")
    return jnp.einsum("pr,prl->pl", gain * total / windows, basis, precision=highest)


def solution(mesh):
    in_specs = (P("pair", "tm", None), P(), P())
    out_specs = P("pair", None)
    return jax.shard_map(local, mesh=mesh, in_specs=in_specs, out_specs=out_specs, check_vma=False)
```

profile of v0, /device:TPU:0, one launch (start us, length us, event | category | flops | bytes accessed | tf_op | source)
XLA Modules:
  0.0 754.4 jit_solution(5621132792303289225)
XLA Ops:
  6.5 0.7 broadcast_subtract_fusion
  8.2 16.8 %cosine_convert_fusion = (bf16[2048,512]{1,0:T(8,128)(2,1)S(1)}, bf16[2048,512]{1,0:T(8,128)(2,1)S(1)}) fusion(s32[512]{0:T(512)S(1)} %iota_add_fusion.1), kind=kLoop, calls=%fused_computation.41 | loop fusion | flops 16777216 | bytes 4196352 | tf_op jit(solution)/shard_map/convert.7
  25.1 4.5 fusion.24
  30.0 0.7 multiply_convert_fusion.1
  30.6 0.6 copy.41
  31.2 0.6 copy.42
  31.8 1.2 convolution_convert_fusion
  33.0 3.5 copy.43
  36.5 5.4 all-to-all-start
  42.4 0.7 constant_dynamic-slice_fusion
  44.0 1.3 gather_fusion.2
  45.2 1.3 gather_fusion
  46.6 18.9 %fusion.29 = (f32[512,2048]{1,0:T(8,128)}, f32[512,2048]{1,0:T(8,128)}) fusion(s32[2048]{0:T(1024)S(1)} %iota_add_fusion, s32[512]{0:T(512)S(1)} %iota_add_fusion.1), kind=kLoop, calls=%fused_computation.50 | loop fusion | flops 15728640 | bytes 8398848 | tf_op jit(solution)/shard_map/cos | solution.py:26
  65.5 14.9 %all-to-all-done = bf16[8,12,16,1024]{3,2,1,0:T(8,128)(2,1)S(1)} async-done(((bf16[8,12,16,1024]{3,2,1,0:T(8,128)(2,1)}), bf16[8,12,16,1024]{3,2,1,0:T(8,128)(2,1)S(1)}, u32[]{:S(2)}, u32[]{:S(2)}) %all-to-all-start) | async-done | bytes 3145760 | tf_op jit(solution)/shard_map/all_to_all | solution.py:83
  80.4 2.8 gather_fusion.3
  83.2 2.8 gather_fusion.1
  85.9 7.2 fusion.19
  93.2 4.9 fusion.18
  98.0 2.6 add_convert_fusion
  100.7 14.6 %fusion.12 = f32[128,16,2048]{2,0,1:T(8,128)} fusion(f32[512,2048]{1,0:T(8,128)} %get-tuple-element.21, f32[512,2048]{1,0:T(8,128)S(1)} %copy-done.4, bf16[128,16,512]{2,0,1:T(8,128)(2,1)S(1)} %get-tuple-element.17, bf16[128,16,512]{2,0,1:T(8,128)(2,1)S(1)} %get-tuple-element.16), kind=kOutput, calls=%fused_computation.26 | convolution fusion | flops 8604614656 | bytes 29360128 | tf_op jit(solution)/shard_map/pwf,fl->pwl/dot_general | solution.py:88
  115.3 16.6 %fusion.33 = f32[128,16,16]{0,2,1:T(8,128)S(1)} fusion(f32[128,16,2048]{2,0,1:T(8,128)} %fusion.12, f32[16,2048]{1,0:T(8,128)S(1)} %copy-done), kind=kOutput, calls=%fused_computation.63 | convolution fusion | flops 805306368 | bytes 17039360 | tf_op jit(solution)/shard_map/pwl,rl->pwr/dot_general | solution.py:89
  132.5 32.3 %fusion = f32[128,16,2048]{2,1,0:T(8,128)} fusion(f32[128,16,16]{1,2,0:T(8,128)S(1)} %copy.46, f32[128,16,2048]{2,0,1:T(8,128)} %fusion.12), kind=kOutput, calls=%fused_computation.4 | convolution fusion | flops 805306368 | bytes 33685504 | tf_op jit(solution)/shard_map/pwr,pwl->prl/dot_general | solution.py:90
  164.9 2.2 multiply_reduce_fusion
  167.1 218.0 %all-reduce.3.cloned.1.call-done = f32[128,16,2048]{2,1,0:T(8,128)} async-done(((f32[128,16,2048]{2,1,0:T(8,128)}), f32[128,16,2048]{2,1,0:T(8,128)}) %all-reduce.3.cloned.1.call-update) | async-done | bytes 16777232 | tf_op jit(solution)/shard_map/psum | solution.py:91
  385.1 25.8 %fusion.50 = f32[128,16,16]{2,1,0:T(8,128)S(1)} fusion(f32[128,16,2048]{2,1,0:T(8,128)} %all-reduce.3.cloned.1.call-done), kind=kOutput, calls=%fused_computation.116 | convolution fusion | flops 805306368 | bytes 16908288 | tf_op jit(solution)/shard_map/prl,psl->prs/dot_general | solution.py:54
  411.4 187.6 %custom-call.7 = f32[128,16,16]{2,1,0:T(8,128)S(1)} custom-call(f32[128,16,16]{2,1,0:T(8,128)S(1)} %fusion.30), custom_call_target="Cholesky" | custom-call | tf_op jit(solution)/shard_map/jit(cholesky)/cholesky | solution.py:55
  599.7 2.7 custom-call.8
  602.9 21.5 %fusion.51 = f32[128,16,2048]{2,1,0:T(8,128)} fusion(f32[128,16,16]{2,1,0:T(8,128)S(1)} %copy.51, f32[128,16,2048]{2,1,0:T(8,128)} %all-reduce.3.cloned.1.call-done), kind=kOutput, calls=%fused_computation.117 | convolution fusion | flops 805306368 | bytes 33685504 | tf_op jit(solution)/shard_map/triangular_solve | solution.py:56
  624.3 35.2 %multiply_reduce_fusion.1 = (f32[128,16]{1,0:T(8,128)S(1)}, f32[128,16]{1,0:T(8,128)S(1)}) fusion(f32[128,16,2048]{2,1,0:T(8,128)} %fusion.51, f32[128,16,2048]{2,0,1:T(8,128)} %fusion.12), kind=kOutput, calls=%fused_computation.58 | convolution fusion | flops 805400576 | bytes 33570816 | tf_op jit(solution)/shard_map/pwl,prl->pwr/dot_general | solution.py:93
  659.6 74.8 %all-reduce = (f32[128,16]{1,0:T(8,128)S(1)}, f32[128,16]{1,0:T(8,128)S(1)}, f32[128]{0:T(128)S(1)}) all-reduce(f32[128,16]{1,0:T(8,128)S(1)} %get-tuple-element.8, f32[128,16]{1,0:T(8,128)S(1)} %get-tuple-element.6, f32[128]{0:T(128)S(1)} %multiply_reduce_fusion), channel_id=1, replica_groups=mesh['pair'=8,'tm'=16] {'tm'}, use_global_device_ids=true, to_apply=%region_13.16 | all-reduce | flops 4224 | bytes 33792 | tf_op jit(solution)/shard_map/psum | solution.py:94
  734.5 11.5 %fusion.52 = f32[128,1,2048]{2,1,0:T(1,128)S(1)} fusion(f32[128,16,1]{1,2,0:T(1,128)S(1)} %bitcast.79, f32[128,16,2048]{2,1,0:T(8,128)} %fusion.51), kind=kOutput, calls=%fused_computation.118 | convolution fusion | flops 50331648 | bytes 17833984 | tf_op jit(solution)/shard_map/pr,prl->pl/dot_general | solution.py:97
  746.1 1.3 copy.69
  (49 shorter events, 5.0 us)
Async XLA Ops:
  6.5 108.8 %copy-start = (f32[16,2048]{1,0:T(8,128)S(1)}, f32[16,2048]{1,0:T(8,128)}, u32[]{:S(2)}) copy-start(f32[16,2048]{1,0:T(8,128)} %param.9) | copy-start | bytes 393220
  8.2 16.8 %copy-start.5 = (bf16[64,16,2048]{2,1,0:T(8,128)(2,1)S(1)}, bf16[64,16,2048]{2,1,0:T(8,128)(2,1)}, u32[]{:S(2)}) copy-start(bf16[64,16,2048]{2,1,0:T(8,128)(2,1)} %param.7) | copy-start | bytes 12582916
  36.5 43.8 %all-to-all-start = ((bf16[8,12,16,1024]{3,2,1,0:T(8,128)(2,1)}), bf16[8,12,16,1024]{3,2,1,0:T(8,128)(2,1)S(1)}, u32[]{:S(2)}, u32[]{:S(2)}) async-start(bf16[8,12,16,1024]{3,2,1,0:T(8,128)(2,1)} %copy.43), calls=%async_computation | async-start | bytes 6291456 | tf_op jit(solution)/shard_map/all_to_all | solution.py:83
  41.9 343.1 %all-reduce.3.cloned.1.call-start = ((), (), s32[]{:S(2)}) async-start(), calls=%async_computation.1 | async-start | bytes 33554432 | tf_op jit(solution)/shard_map/psum | solution.py:91
  85.9 7.2 copy-start.2
  98.0 2.7 copy-start.4
  100.7 14.7 %copy-start.3 = (bf16[128,16,512]{2,0,1:T(8,128)(2,1)}, bf16[128,16,512]{2,0,1:T(8,128)(2,1)S(1)}, u32[]{:S(2)}) copy-start(bf16[128,16,512]{2,0,1:T(8,128)(2,1)S(1)} %get-tuple-element.17) | copy-start | bytes 6291460
  734.5 12.9 %copy-start.1 = (f32[16,2048]{1,0:T(8,128)S(1)}, f32[16,2048]{1,0:T(8,128)}, u32[]{:S(2)}) copy-start(f32[16,2048]{1,0:T(8,128)} %param.9) | copy-start | bytes 393220
Sparse Core Ops, SparseCore 0:
  165.0 220.0 all-reduce.2
where the time goes:
time: 764 us; the launch traced here: 754 us
  other arithmetic  246 us (32%)
  waiting for transfers between devices  233 us (30%)
  matrix products  163 us (21%)
  blocking collectives  74.8 us (10%)
  local copies, waits for them, and re-layouts  17.5 us (2%)
  between operations  13.9 us (2%)
    psum x1, waiting for transfers between devices, local(): raw, energy = lax.psum((partial_raw, energy_local), 'tm')  218 us
    another operation x4, other arithmetic, orthonormal(): lower = jnp.linalg.cholesky(gram)  188 us
    psum x1, blocking collectives, local(): lax.psum((jnp.sum(coeffs, axis=1), jnp.sum(coeffs * coeffs, axis=1)), 'tm')  74.8 us
    dot_general x1, matrix products, local(): coeffs = jnp.einsum('pwl,prl->pwr', lagged, basis, precision=highest)  35.2 us
    dot_general x1, matrix products, local(): partial_raw = jnp.einsum('pwr,pwl->prl', probe, lagged, precision=highest)  32.3 us
    dot_general x1, matrix products, orthonormal(): gram = jnp.einsum('prl,psl->prs', raw, raw, precision=highest)  25.8 us
    another operation x1, matrix products, orthonormal(): return lax.linalg.triangular_solve(lower, raw, left_side=True, lower=True)  21.5 us
    another operation x3, other arithmetic  20.1 us
  transfers between devices with their start and end apart: 2, of which 2 were waited for; matrix products, arithmetic and copies ran while one was open for 3% of the time, Pallas kernels for 0%

commit v1 on v0

v1 whole, which is shorter than its diff:
```python
import math

import jax
import jax.numpy as jnp
import numpy as np
from jax import lax
from jax.experimental import pallas as pl
from jax.experimental.pallas import tpu as pltpu
from jax.sharding import PartitionSpec as P

SAMPLES = 2048
NF = 512
LAGS = 2048
RANK = 16
CAP = 12
PAIRS_DEV = 128
F0 = NF // 2
STEP = 32
ISTEP = 16
F32 = jnp.float32
BF16 = jnp.bfloat16


def turns(first, second):
    k = np.mod(np.asarray(first)[:, None] * np.asarray(second)[None, :], SAMPLES)
    return k.astype(np.float64) * (2.0 * math.pi / SAMPLES)


def table_parts():
    freq = F0 + np.arange(NF)
    base = turns(np.arange(0, SAMPLES // 2, STEP), freq)
    step = turns(np.arange(STEP), freq)
    forward = (np.stack([np.cos(base), np.sin(base)]), np.stack([np.cos(step), np.sin(step)]))
    shifts = np.arange(LAGS) - LAGS // 2
    ibase = turns(F0 + np.arange(0, NF, ISTEP), shifts)
    istep = turns(np.arange(ISTEP), shifts)
    inverse = (
        np.stack([np.cos(ibase), np.sin(ibase)]) / math.sqrt(NF),
        np.stack([np.cos(istep), np.sin(istep)]),
    )
    return tuple(p.astype(np.float32) for p in forward + inverse)


def gram_excess():
    freq = F0 + np.arange(NF)
    shifts = np.arange(LAGS) - LAGS // 2
    angle = np.mod(freq[:, None] * shifts[None, :], SAMPLES).astype(np.float32)
    angle = angle * np.float32(2.0 * math.pi / SAMPLES)
    root = np.float32(math.sqrt(NF))
    blocks = []
    for wave in (np.cos(angle), -np.sin(angle)):
        rows = (wave / root).astype(jnp.bfloat16).astype(np.float64)
        blocks.append(rows @ rows.T - 2.0 * np.eye(NF))
    return np.stack(blocks).astype(np.float32).astype(jnp.bfloat16)


def split3(x):
    high = x.astype(BF16)
    rest = x - high.astype(F32)
    mid = rest.astype(BF16)
    low = (rest - mid.astype(F32)).astype(BF16)
    return jnp.concatenate([high, mid, low], axis=0)


def split2(x):
    high = x.astype(BF16)
    return jnp.concatenate([high, (x - high.astype(F32)).astype(BF16)], axis=0)


def sum3(x):
    n = x.shape[0] // 3
    return x[:n] + x[n : 2 * n] + x[2 * n :]


def dot_nt(a, b, precision=None):
    return lax.dot_general(
        a, b, (((1,), (1,)), ((), ())), preferred_element_type=F32, precision=precision
    )


def dot_nn(a, b):
    return jnp.dot(a, b, preferred_element_type=F32)


def whiten_kernel(sel_ref, rec_ref, base_ref, step_ref, out_ref, table, white):
    i = pl.program_id(0)

    @pl.when(i == 0)
    def _():
        parity = lax.broadcasted_iota(jnp.int32, (1, NF), 1) & 1
        sign = 1.0 - 2.0 * parity.astype(F32)
        cos_step = step_ref[0]
        sin_step = step_ref[1]

        def body(n, carry):
            cos_base = base_ref[0, pl.ds(n, 1), :]
            sin_base = base_ref[1, pl.ds(n, 1), :]
            cos = cos_base * cos_step - sin_base * sin_step
            sin = sin_base * cos_step + cos_base * sin_step
            row = pl.multiple_of(n * STEP, STEP)
            far = pl.multiple_of(n * STEP + SAMPLES // 2, STEP)
            table[pl.ds(row, STEP), :NF] = cos.astype(BF16)
            table[pl.ds(row, STEP), NF:] = sin.astype(BF16)
            table[pl.ds(far, STEP), :NF] = (cos * sign).astype(BF16)
            table[pl.ds(far, STEP), NF:] = (sin * sign).astype(BF16)
            return carry

        lax.fori_loop(0, SAMPLES // 2 // STEP, body, 0)

    spectra = dot_nn(rec_ref[...], table[...])
    re = spectra[:, :NF]
    im = spectra[:, NF:]
    power = re * re + im * im
    level = jnp.mean(power, axis=1, keepdims=True)
    factor = lax.rsqrt(power + level + 1e-06)
    rows = jnp.concatenate([re * factor, im * factor], axis=1).astype(BF16)
    channels, windows, width = white.shape
    per = rec_ref.shape[0] // windows
    white[pl.ds(i * per, per)] = rows.reshape(per, windows, width)

    @pl.when(i == pl.num_programs(0) - 1)
    def _():
        def body(n, carry):
            out_ref[n] = white[sel_ref[n]]
            return carry

        lax.fori_loop(0, out_ref.shape[0], body, 0)


def whiten(records, sel, base, step):
    ch_dev, win_dev, samples = records.shape
    rows = ch_dev * win_dev
    block = 256
    full = lambda i, sel: (0, 0, 0)
    return pl.pallas_call(
        whiten_kernel,
        out_shape=jax.ShapeDtypeStruct((sel.shape[0], win_dev, 2 * NF), BF16),
        grid_spec=pltpu.PrefetchScalarGridSpec(
            num_scalar_prefetch=1,
            grid=(rows // block,),
            in_specs=[
                pl.BlockSpec((block, samples), lambda i, sel: (i, 0)),
                pl.BlockSpec(base.shape, full),
                pl.BlockSpec(step.shape, full),
            ],
            out_specs=pl.BlockSpec((sel.shape[0], win_dev, 2 * NF), full),
            scratch_shapes=[
                pltpu.VMEM((samples, 2 * NF), BF16),
                pltpu.VMEM((ch_dev, win_dev, 2 * NF), BF16),
            ],
        ),
        compiler_params=pltpu.CompilerParams(
            dimension_semantics=("arbitrary",), vmem_limit_bytes=48 << 20
        ),
        name="whiten",
    )(sel, records.reshape(rows, samples), base, step)


def inverse_kernel(sketch_ref, base_ref, step_ref, inv_ref, s3_ref):
    cos_step = step_ref[0]
    sin_step = step_ref[1]

    def body(n, carry):
        cos_base = base_ref[0, pl.ds(n, 1), :]
        sin_base = base_ref[1, pl.ds(n, 1), :]
        cos = cos_base * cos_step - sin_base * sin_step
        sin = sin_base * cos_step + cos_base * sin_step
        row = pl.multiple_of(n * ISTEP, ISTEP)
        low = pl.multiple_of(n * ISTEP + NF, ISTEP)
        inv_ref[pl.ds(row, ISTEP), :] = cos.astype(BF16)
        inv_ref[pl.ds(low, ISTEP), :] = (-sin).astype(BF16)
        return carry

    lax.fori_loop(0, NF // ISTEP, body, 0)
    s3_ref[...] = split3(sum3(dot_nt(split3(sketch_ref[...]), inv_ref[...])))


def inverse_table(sketch, base, step):
    return pl.pallas_call(
        inverse_kernel,
        out_shape=(
            jax.ShapeDtypeStruct((2 * NF, LAGS), BF16),
            jax.ShapeDtypeStruct((3 * RANK, 2 * NF), BF16),
        ),
        compiler_params=pltpu.CompilerParams(vmem_limit_bytes=32 << 20),
        name="inverse_table",
    )(sketch, base, step)


def cross_kernel(slot_ref, arr_ref, out_ref):
    i = pl.program_id(0)
    group = out_ref.shape[1]
    for q in range(group):
        left = arr_ref[slot_ref[0, i * group + q]].astype(F32)
        right = arr_ref[slot_ref[1, i * group + q]].astype(F32)
        lre, lim = left[:, :NF], left[:, NF:]
        rre, rim = right[:, :NF], right[:, NF:]
        out_ref[0, q, :, :NF] = (lre * rre + lim * rim).astype(BF16)
        out_ref[0, q, :, NF:] = (lim * rre - lre * rim).astype(BF16)


def correlate(slots, arrived, parts):
    windows = arrived.shape[1]
    group = PAIRS_DEV // parts
    return pl.pallas_call(
        cross_kernel,
        out_shape=jax.ShapeDtypeStruct((parts, group, windows, 2 * NF), BF16),
        grid_spec=pltpu.PrefetchScalarGridSpec(
            num_scalar_prefetch=1,
            grid=(parts,),
            in_specs=[pl.BlockSpec(arrived.shape, lambda i, s: (0, 0, 0))],
            out_specs=pl.BlockSpec((1, group, windows, 2 * NF), lambda i, s: (i, 0, 0, 0)),
        ),
        compiler_params=pltpu.CompilerParams(
            dimension_semantics=("arbitrary",), vmem_limit_bytes=32 << 20
        ),
        name="cross",
    )(slots, arrived)


def stack_kernel(c_ref, s3_ref, e_ref, o_ref, r_s, h_s, y_s, g_s, en_s):
    parts, group, windows, width = c_ref.shape
    count = parts * windows
    s3 = s3_ref[...]
    probes = []
    for p in range(group):
        c = c_ref[:, p].reshape(count, width)
        probe = sum3(dot_nt(s3, c))
        probes.append(probe)
        r_s[:, p, :] = sum3(dot_nn(split3(probe), c))
        cf = c.astype(F32)
        en_s[pl.ds(p, 1), :] = jnp.sum(cf * cf, axis=0, keepdims=True)
    raw = r_s[...].reshape(RANK * group, width)
    raw2 = split2(raw)
    rows = RANK * group
    for half in range(2):
        lanes = slice(half * NF, (half + 1) * NF)
        more = dot_nn(raw2[:, lanes], e_ref[half])
        full = 2.0 * raw[:, lanes] + (more[:rows] + more[rows:])
        h_s[:, :, lanes] = full.reshape(RANK, group, NF)
    lane = lax.broadcasted_iota(jnp.int32, (RANK, 128), 1)
    row = lax.broadcasted_iota(jnp.int32, (RANK, 128), 0)
    unit = (lane == row + RANK).astype(F32)
    for p in range(group):
        c = c_ref[:, p].reshape(count, width)
        y = sum3(dot_nt(split3(h_s[:, p, :]), c))
        gram = dot_nt(y, probes[p], lax.Precision.HIGHEST)
        y_s[:, p, :] = y
        g_s[:, p, :] = unit
        g_s[:, p, :RANK] = gram
    ys = [y_s[r] for r in range(RANK)]
    gs = [g_s[r] for r in range(RANK)]
    for k in range(RANK):
        pivot = gs[k][:, k : k + 1]
        scale = lax.rsqrt(pivot)
        scale = scale * (1.5 - 0.5 * pivot * scale * scale)
        gs[k] = gs[k] * scale
        ys[k] = ys[k] * scale
        for r in range(k + 1, RANK):
            factor = gs[r][:, k : k + 1] * scale
            gs[r] = gs[r] - factor * gs[k]
            ys[r] = ys[r] - factor * ys[k]
    energy = jnp.sum(en_s[...], axis=1, keepdims=True)
    mix = jnp.zeros_like(gs[0])
    for r in range(RANK):
        power = jnp.sum(ys[r] * ys[r], axis=1, keepdims=True)
        total = jnp.sum(ys[r], axis=1, keepdims=True)
        gain = power / (power + energy / (2 * NF))
        mix = mix + (gain * total / count) * gs[r]
    stack = jnp.zeros((group, width), F32)
    for r in range(RANK):
        stack = stack + mix[:, RANK + r : RANK + r + 1] * r_s[r]
    for t in range(parts):
        o_ref[t] = stack


def stack_up(cross, s3, excess):
    parts, group, windows, width = cross.shape
    return pl.pallas_call(
        stack_kernel,
        out_shape=jax.ShapeDtypeStruct((parts, group, width), F32),
        scratch_shapes=[
            pltpu.VMEM((RANK, group, width), F32),
            pltpu.VMEM((RANK, group, width), F32),
            pltpu.VMEM((RANK, group, parts * windows), F32),
            pltpu.VMEM((RANK, group, 128), F32),
            pltpu.VMEM((group, width), F32),
        ],
        compiler_params=pltpu.CompilerParams(vmem_limit_bytes=48 << 20),
        name="stack",
    )(cross, s3, excess)


def lags_kernel(x_ref, inv_ref, o_ref, x2):
    rows = x_ref.shape[0]

    @pl.when(pl.program_id(0) == 0)
    def _():
        x2[...] = split2(x_ref[...])

    y = dot_nn(x2[...], inv_ref[...])
    o_ref[...] = y[:rows] + y[rows:]


def to_lags(x, inverse):
    rows, width = x.shape
    block = 512
    return pl.pallas_call(
        lags_kernel,
        out_shape=jax.ShapeDtypeStruct((rows, LAGS), F32),
        grid=(LAGS // block,),
        in_specs=[
            pl.BlockSpec((rows, width), lambda i: (0, 0)),
            pl.BlockSpec((width, block), lambda i: (0, i)),
        ],
        out_specs=pl.BlockSpec((rows, block), lambda i: (0, i)),
        scratch_shapes=[pltpu.VMEM((2 * rows, width), BF16)],
        compiler_params=pltpu.CompilerParams(
            dimension_semantics=("arbitrary",), vmem_limit_bytes=32 << 20
        ),
        name="lags",
    )(x, inverse)


def local(records, pair_list, sketch):
    base, step, ibase, istep = table_parts()
    n_pair = lax.axis_size("pair")
    n_tm = lax.axis_size("tm")
    owner = lax.axis_index("pair")
    ch_dev, win_dev, _ = records.shape

    wanted = pair_list.reshape(n_pair, 2 * PAIRS_DEV) - owner * ch_dev
    column = jnp.arange(ch_dev)
    asked = jnp.any(wanted[:, :, None] == column[None, None, :], axis=1)
    before = jnp.sum(asked[:, :, None] & (column[:, None] < column[None, :]), axis=1)
    slot = jnp.arange(CAP)
    picked = asked[:, None, :] & (before[:, None, :] == slot[None, :, None])
    sel = jnp.sum(jnp.where(picked, column, 0), axis=2).astype(jnp.int32).reshape(-1)
    outgoing = whiten(records, sel, base, step)

    mine = lax.dynamic_slice_in_dim(pair_list, owner * PAIRS_DEV, PAIRS_DEV, 0).T
    everyone = jnp.arange(n_pair * ch_dev)
    held = jnp.any(mine.reshape(-1)[:, None] == everyone[None, :], axis=0)
    block = mine // ch_dev
    first = (block * ch_dev)[:, :, None]
    ahead = held & (everyone >= first) & (everyone < mine[:, :, None])
    slots = (block * CAP + jnp.sum(ahead, axis=2)).astype(jnp.int32)

    arrived = lax.all_to_all(
        outgoing.reshape(n_pair, CAP, win_dev, 2 * NF), "pair", 0, 0, tiled=True
    ).reshape(n_pair * CAP, win_dev, 2 * NF)
    inverse, s3 = inverse_table(sketch, ibase, istep)
    cross = correlate(slots, arrived, n_tm)
    cross = lax.all_to_all(cross, "tm", 0, 0, tiled=True)
    stack = stack_up(cross, s3, gram_excess())
    stack = lax.all_to_all(stack, "tm", 0, 0, tiled=True)
    return to_lags(stack.reshape(PAIRS_DEV, 2 * NF), inverse)


def solution(mesh):
    in_specs = (P("pair", "tm", None), P(), P())
    out_specs = P("pair", None)
    return jax.shard_map(local, mesh=mesh, in_specs=in_specs, out_specs=out_specs, check_vma=False)
```

time: 764 us -> 164 us (0.21); the launches traced: 754 us -> 163 us
  other arithmetic: 246 us -> 2.48 us
  matrix products: 163 us -> 0 us
  waiting for transfers between devices: 233 us -> 94.3 us
  blocking collectives: 74.8 us -> 14.6 us
  Pallas kernels: 0 us -> 30.3 us
  between operations: 13.9 us -> 0.14 us
  local copies, waits for them, and re-layouts: 17.5 us -> 8.73 us
    psum x1 -> x0, waiting for transfers between devices: 218 us -> none  [local(): raw, energy = lax.psum((partial_raw, energy_local), 'tm')]
    another operation x12 -> x0, other arithmetic: 211 us -> none  [the longest x4 188 us: orthonormal(): lower = jnp.linalg.cholesky(gram)]
    dot_general x8 -> x0, matrix products: 142 us -> none  [the longest x1 35.2 us: local(): coeffs = jnp.einsum('pwl,prl->pwr', lagged, basis, precision=highest)]
    all_to_all x1 -> x2, waiting for transfers between devices: 14.9 us -> 94.3 us  [the longest x1 57.7 us: local(): cross = lax.all_to_all(cross, 'tm', 0, 0, tiled=True)]
    psum x1 -> x0, blocking collectives: 74.8 us -> none  [local(): lax.psum((jnp.sum(coeffs, axis=1), jnp.sum(coeffs * coeffs, axis=1)), 'tm')]
    pallas_call x0 -> x5, Pallas kernels: none -> 30.3 us  [the longest x1 12.9 us: stack_up(): pl.pallas_call(stack_kernel, out_shape=jax.ShapeDtypeStruct((parts, group...]
    another operation x1 -> x0, matrix products: 21.5 us -> none  [orthonormal(): return lax.linalg.triangular_solve(lower, raw, left_side=True, lower=True)]
    cos x1 -> x0, other arithmetic: 18.9 us -> none  [tables(): jnp.cos(angle)]
  transfers between devices with their start and end apart: 2 -> 2, of which waited for: 2 -> 2; matrix products, arithmetic and copies ran while one was open for 3% -> 1% of each run, Pallas kernels for 0% -> 2%
where the time goes in v1:
time: 164 us; the launch traced here: 163 us
  waiting for transfers between devices  94.3 us (58%)
  Pallas kernels  30.3 us (18%)
  blocking collectives  14.6 us (9%)
  starting transfers between devices  12.6 us (8%)
  local copies, waits for them, and re-layouts  8.73 us (5%)
  other arithmetic  2.48 us (2%)
    all_to_all x1, waiting for transfers between devices, local(): cross = lax.all_to_all(cross, 'tm', 0, 0, tiled=True)  57.7 us
    all_to_all x1, waiting for transfers between devices, local(): lax.all_to_all(outgoing.reshape(n_pair, CAP, win_dev, 2 * NF), 'pair', 0,...  36.6 us
    all_to_all x1, blocking collectives, local(): stack = lax.all_to_all(stack, 'tm', 0, 0, tiled=True)  14.6 us
    pallas_call x1, Pallas kernels, stack_up(): pl.pallas_call(stack_kernel, out_shape=jax.ShapeDtypeStruct((parts, group...  12.9 us
    pallas_call x1, Pallas kernels, whiten(): pl.pallas_call(whiten_kernel, out_shape=jax.ShapeDtypeStruct((sel.shape[0...  8.96 us
    unnamed x20, local copies, waits for them, and re-layouts  7.39 us
    all_to_all x1, starting transfers between devices, local(): cross = lax.all_to_all(cross, 'tm', 0, 0, tiled=True)  7.23 us
    all_to_all x1, starting transfers between devices, local(): lax.all_to_all(outgoing.reshape(n_pair, CAP, win_dev, 2 * NF), 'pair', 0,...  5.4 us
  transfers between devices with their start and end apart: 2, of which 2 were waited for; matrix products, arithmetic and copies ran while one was open for 1% of the time, Pallas kernels for 2%

profile of v1, /device:TPU:0, one launch (start us, length us, event | category | flops | bytes accessed | tf_op | source)
XLA Modules:
  0.0 163.2 jit_solution(3955194057706302444)
XLA Ops:
  0.0 0.7 broadcast_subtract_fusion
  0.7 0.2 copy.10
  1.0 0.3 sub.22
  1.2 0.2 fusion.3
  1.5 0.1 convert_reduce_fusion.1
  1.6 0.3 select_reduce_fusion
  1.9 0.1 copy.11
  2.0 0.1 reshape.42.sel_ref
  2.1 0.9 copy-done.7
  3.0 0.9 copy-done.8
  3.9 9.0 %whiten.1 = bf16[96,16,1024]{2,1,0:T(8,128)(2,1)S(1)} custom-call(s32[96]{0:T(128)S(1)} %reshape.42.sel_ref, bf16[1024,2048]{1,0:T(8,128)(2,1)} %bitcast.13, f32[2,32,512]{2,1,0:T(8,128)S(1)} %copy-done.8, f32[2,32,512]{2,1,0:T(8,128)S(1)} %copy-done.7), custom_call_target="tpu_custom_call" | custom-call | tf_op jit(solution)/shard_map/whiten/pallas_call | solution.py:135
  12.8 0.0 copy-start.1
  12.9 1.6 %copy-done.1 = bf16[96,16,1024]{2,1,0:T(8,128)(2,1)} copy-done((bf16[96,16,1024]{2,1,0:T(8,128)(2,1)}, bf16[96,16,1024]{2,1,0:T(8,128)(2,1)S(1)}, u32[]{:S(2)}) %copy-start.1) | copy-done | bytes 3145752
  14.5 5.4 %all-to-all-start = ((bf16[8,12,16,1024]{3,2,1,0:T(8,128)(2,1)}), bf16[8,12,16,1024]{3,2,1,0:T(8,128)(2,1)S(1)}, u32[]{:S(2)}, u32[]{:S(2)}) async-start(bf16[8,12,16,1024]{3,2,1,0:T(8,128)(2,1)} %bitcast.11), calls=%async_computation | async-start | bytes 6291456 | tf_op jit(solution)/shard_map/all_to_all | solution.py:349
  19.9 0.7 dynamic-slice_bitcast_fusion
  20.6 0.7 broadcast_multiply_fusion
  21.3 0.1 fusion
  21.4 0.3 convert_reduce_fusion
  21.7 36.6 %all-to-all-done = bf16[8,12,16,1024]{3,2,1,0:T(8,128)(2,1)S(1)} async-done(((bf16[8,12,16,1024]{3,2,1,0:T(8,128)(2,1)}), bf16[8,12,16,1024]{3,2,1,0:T(8,128)(2,1)S(1)}, u32[]{:S(2)}, u32[]{:S(2)}) %all-to-all-start) | async-done | bytes 3145760 | tf_op jit(solution)/shard_map/all_to_all | solution.py:349
  58.3 2.3 %cross.1 = bf16[16,8,16,1024]{3,2,1,0:T(8,128)(2,1)S(1)} custom-call(s32[2,128]{1,0:T(2,128)S(1)} %multiply_add_fusion.slot_ref, bf16[96,16,1024]{2,1,0:T(8,128)(2,1)S(1)} %bitcast.10), custom_call_target="tpu_custom_call" | custom-call | tf_op jit(solution)/shard_map/cross/pallas_call | solution.py:205
  60.6 0.0 copy-start
  60.7 2.0 %copy-done = bf16[16,8,16,1024]{3,2,1,0:T(8,128)(2,1)} copy-done((bf16[16,8,16,1024]{3,2,1,0:T(8,128)(2,1)}, bf16[16,8,16,1024]{3,2,1,0:T(8,128)(2,1)S(1)}, u32[]{:S(2)}) %copy-start) | copy-done | bytes 4194328
  62.6 7.2 %all-to-all-start.1 = ((bf16[16,8,16,1024]{3,2,1,0:T(8,128)(2,1)}), bf16[16,8,16,1024]{3,2,1,0:T(8,128)(2,1)}, u32[]{:S(2)}, u32[]{:S(2)}) async-start(bf16[16,8,16,1024]{3,2,1,0:T(8,128)(2,1)} %copy-done), calls=%async_computation.1 | async-start | bytes 8388608 | tf_op jit(solution)/shard_map/all_to_all | solution.py:354
  69.9 0.0 copy-done.5
  69.9 0.0 copy-done.6
  69.9 0.0 copy-done.9
  69.9 3.0 %inverse_table.1 = (bf16[1024,2048]{1,0:T(8,128)(2,1)S(1)}, bf16[48,1024]{1,0:T(8,128)(2,1)S(1)}) custom-call(f32[16,2048]{1,0:T(8,128)S(1)} %copy-done.9, f32[2,32,2048]{2,1,0:T(8,128)S(1)} %copy-done.5, f32[2,16,2048]{2,1,0:T(8,128)S(1)} %copy-done.6), custom_call_target="tpu_custom_call" | custom-call | tf_op jit(solution)/shard_map/inverse_table/pallas_call | solution.py:179
  72.9 1.9 %copy-done.2 = bf16[1024,2048]{1,0:T(8,128)(2,1)} copy-done((bf16[1024,2048]{1,0:T(8,128)(2,1)}, bf16[1024,2048]{1,0:T(8,128)(2,1)S(1)}, u32[]{:S(2)}) %copy-start.2) | copy-done | bytes 4194328
  74.8 57.7 %all-to-all-done.1.c_ref = bf16[16,8,16,1024]{3,2,1,0:T(8,128)(2,1)} async-done(((bf16[16,8,16,1024]{3,2,1,0:T(8,128)(2,1)}), bf16[16,8,16,1024]{3,2,1,0:T(8,128)(2,1)}, u32[]{:S(2)}, u32[]{:S(2)}) %all-to-all-start.1) | async-done | bytes 4194336 | tf_op jit(solution)/shard_map/all_to_all | solution.py:354
  132.5 12.9 %stack.1 = f32[16,8,1024]{2,1,0:T(8,128)S(1)} custom-call(bf16[16,8,16,1024]{3,2,1,0:T(8,128)(2,1)} %all-to-all-done.1.c_ref, bf16[48,1024]{1,0:T(8,128)(2,1)S(1)} %get-tuple-element.7.s3_ref, bf16[2,512,512]{2,1,0:T(8,128)(2,1)S(1)} %copy-done.4), custom_call_target="tpu_custom_call" | custom-call | tf_op jit(solution)/shard_map/stack/pallas_call | solution.py:279
  145.5 14.6 %all_to_all.15 = f32[16,8,1024]{2,1,0:T(8,128)S(1)} all-to-all(f32[16,8,1024]{2,1,0:T(8,128)S(1)} %stack.1), channel_id=1, replica_groups=mesh['pair'=8,'tm'=16] {'tm'}, dimensions={0} | all-to-all | bytes 1048576 | tf_op jit(solution)/shard_map/all_to_all | solution.py:356
  160.1 3.1 %lags.1 = f32[128,2048]{1,0:T(8,128)} custom-call(f32[128,1024]{1,0:T(8,128)S(1)} %bitcast.12, bf16[1024,2048]{1,0:T(8,128)(2,1)S(1)} %copy-done.3), custom_call_target="tpu_custom_call" | custom-call | tf_op jit(solution)/shard_map/lags/pallas_call | solution.py:308
  (12 shorter events, 0.0 us)
Async XLA Ops:
  2.1 0.9 copy-start.7
  3.0 0.9 copy-start.8
  12.8 1.7 %copy-start.1 = (bf16[96,16,1024]{2,1,0:T(8,128)(2,1)}, bf16[96,16,1024]{2,1,0:T(8,128)(2,1)S(1)}, u32[]{:S(2)}) copy-start(bf16[96,16,1024]{2,1,0:T(8,128)(2,1)S(1)} %whiten.1) | copy-start | bytes 9437188
  14.5 43.8 %all-to-all-start = ((bf16[8,12,16,1024]{3,2,1,0:T(8,128)(2,1)}), bf16[8,12,16,1024]{3,2,1,0:T(8,128)(2,1)S(1)}, u32[]{:S(2)}, u32[]{:S(2)}) async-start(bf16[8,12,16,1024]{3,2,1,0:T(8,128)(2,1)} %bitcast.11), calls=%async_computation | async-start | bytes 6291456 | tf_op jit(solution)/shard_map/all_to_all | solution.py:349
  60.6 2.0 %copy-start = (bf16[16,8,16,1024]{3,2,1,0:T(8,128)(2,1)}, bf16[16,8,16,1024]{3,2,1,0:T(8,128)(2,1)S(1)}, u32[]{:S(2)}) copy-start(bf16[16,8,16,1024]{3,2,1,0:T(8,128)(2,1)S(1)} %cross.1) | copy-start | bytes 12582916
  62.6 7.3 %copy-start.5 = (f32[2,32,2048]{2,1,0:T(8,128)S(1)}, f32[2,32,2048]{2,1,0:T(8,128)}, u32[]{:S(2)}) copy-start(f32[2,32,2048]{2,1,0:T(8,128)} %constant.45.clone.base_ref) | copy-start | bytes 1572868
  62.6 7.3 %copy-start.6 = (f32[2,16,2048]{2,1,0:T(8,128)S(1)}, f32[2,16,2048]{2,1,0:T(8,128)}, u32[]{:S(2)}) copy-start(f32[2,16,2048]{2,1,0:T(8,128)} %constant.46.clone.step_ref) | copy-start | bytes 786436
  62.6 7.3 %copy-start.9 = (f32[16,2048]{1,0:T(8,128)S(1)}, f32[16,2048]{1,0:T(8,128)}, u32[]{:S(2)}) copy-start(f32[16,2048]{1,0:T(8,128)} %sketch_ref.1) | copy-start | bytes 393220
  62.6 69.9 %copy-start.4 = (bf16[2,512,512]{2,1,0:T(8,128)(2,1)S(1)}, bf16[2,512,512]{2,1,0:T(8,128)(2,1)}, u32[]{:S(2)}) copy-start(bf16[2,512,512]{2,1,0:T(8,128)(2,1)} %constant.47.clone.e_ref) | copy-start | bytes 3145732
  62.6 69.9 %all-to-all-start.1 = ((bf16[16,8,16,1024]{3,2,1,0:T(8,128)(2,1)}), bf16[16,8,16,1024]{3,2,1,0:T(8,128)(2,1)}, u32[]{:S(2)}, u32[]{:S(2)}) async-start(bf16[16,8,16,1024]{3,2,1,0:T(8,128)(2,1)} %copy-done), calls=%async_computation.1 | async-start | bytes 8388608 | tf_op jit(solution)/shard_map/all_to_all | solution.py:354
  72.9 2.0 %copy-start.2 = (bf16[1024,2048]{1,0:T(8,128)(2,1)}, bf16[1024,2048]{1,0:T(8,128)(2,1)S(1)}, u32[]{:S(2)}) copy-start(bf16[1024,2048]{1,0:T(8,128)(2,1)S(1)} %get-tuple-element.8.inv_ref) | copy-start | bytes 12582916
  132.5 27.6 %copy-start.3 = (bf16[1024,2048]{1,0:T(8,128)(2,1)S(1)}, bf16[1024,2048]{1,0:T(8,128)(2,1)}, u32[]{:S(2)}) copy-start(bf16[1024,2048]{1,0:T(8,128)(2,1)} %copy-done.2) | copy-start | bytes 12582916

commit v2 on v1

--- a/solution.py
+++ b/solution.py
@@ -17,6 +17,7 @@
 F0 = NF // 2
 STEP = 32
 ISTEP = 16
+CHUNKS = ((0, 256), (256, 512))
 F32 = jnp.float32
 BF16 = jnp.bfloat16
 
@@ -54,6 +55,10 @@
     return np.stack(blocks).astype(np.float32).astype(jnp.bfloat16)
 
 
+def in_hbm(x):
+    return pltpu.with_memory_space_constraint(x, pltpu.HBM)
+
+
 def split3(x):
     high = x.astype(BF16)
     rest = x - high.astype(F32)
@@ -82,19 +87,51 @@
     return jnp.dot(a, b, preferred_element_type=F32)
 
 
-def whiten_kernel(sel_ref, rec_ref, base_ref, step_ref, out_ref, table, white):
+def cut(rows, lo, hi):
+    return jnp.concatenate([rows[:, lo:hi], rows[:, NF + lo : NF + hi]], axis=1)
+
+
+def pick(pair_ref, owner, channels, peers):
+    shape = (channels, PAIRS_DEV)
+    column = lax.broadcasted_iota(jnp.int32, shape, 0)
+    lane = lax.broadcasted_iota(jnp.int32, shape, 1)
+    asked = jnp.zeros(shape, F32)
+    for d in range(peers):
+        named = pair_ref[:, d * PAIRS_DEV : (d + 1) * PAIRS_DEV] - owner * channels
+        hit = (column == named[0:1]) | (column == named[1:2])
+        seen = jnp.max(hit.astype(F32), axis=1, keepdims=True)
+        asked = jnp.where(lane == d, seen, asked)
+    square = (channels, channels)
+    earlier = lax.broadcasted_iota(jnp.int32, square, 1) < lax.broadcasted_iota(jnp.int32, square, 0)
+    before = dot_nn(earlier.astype(F32).astype(BF16), asked.astype(BF16))
+    number = column.astype(F32) * asked
+    rows = []
+    for k in range(CAP):
+        rows.append(jnp.sum(jnp.where(before == k, number, 0.0), axis=0, keepdims=True))
+    return jnp.concatenate(rows, axis=0).astype(jnp.int32)
+
+
+def whiten_kernel(owner_ref, pair_ref, rec_ref, parts_ref, *rest):
+    count = 1 + (len(CHUNKS) - 1) * (pair_ref.shape[1] // PAIRS_DEV)
+    outs, bufs, rest = rest[:count], rest[count : 2 * count], rest[2 * count :]
+    table, white, chosen, sel_ref, chosen_sem, sems = rest
     i = pl.program_id(0)
+    peers = pair_ref.shape[1] // PAIRS_DEV
+    owner = owner_ref[0]
+    fetch = pltpu.make_async_copy(chosen, sel_ref, chosen_sem)
 
     @pl.when(i == 0)
     def _():
+        chosen[...] = pick(pair_ref, owner, white.shape[0], peers)
+        fetch.start()
         parity = lax.broadcasted_iota(jnp.int32, (1, NF), 1) & 1
         sign = 1.0 - 2.0 * parity.astype(F32)
-        cos_step = step_ref[0]
-        sin_step = step_ref[1]
+        cos_step = parts_ref[2]
+        sin_step = parts_ref[3]
 
         def body(n, carry):
-            cos_base = base_ref[0, pl.ds(n, 1), :]
-            sin_base = base_ref[1, pl.ds(n, 1), :]
+            cos_base = parts_ref[0, pl.ds(n, 1), :]
+            sin_base = parts_ref[1, pl.ds(n, 1), :]
             cos = cos_base * cos_step - sin_base * sin_step
             sin = sin_base * cos_step + cos_base * sin_step
             row = pl.multiple_of(n * STEP, STEP)
@@ -120,40 +157,66 @@
 
     @pl.when(i == pl.num_programs(0) - 1)
     def _():
-        def body(n, carry):
-            out_ref[n] = white[sel_ref[n]]
-            return carry
-
-        lax.fori_loop(0, out_ref.shape[0], body, 0)
-
-
-def whiten(records, sel, base, step):
+        fetch.wait()
+        sends = []
+
+        def fill(buf, row, peer, lo, hi):
+            def body(n, carry):
+                buf[row + n] = cut(white[sel_ref[n, peer]], lo, hi)
+                return carry
+
+            lax.fori_loop(0, CAP, body, 0, unroll=4)
+
+        for d in range(peers):
+            fill(bufs[0], d * CAP, d, *CHUNKS[0])
+        sends.append(pltpu.make_async_copy(bufs[0], outs[0], sems.at[0]))
+        sends[-1].start()
+        for j, (lo, hi) in enumerate(CHUNKS[1:]):
+            for x in range(peers):
+                n = 1 + j * peers + x
+                fill(bufs[n], 0, owner ^ x, lo, hi)
+                sends.append(pltpu.make_async_copy(bufs[n], outs[n], sems.at[n]))
+                sends[-1].start()
+        for send in sends:
+            send.wait()
+
+
+def whiten(records, pairs, owner, parts):
     ch_dev, win_dev, samples = records.shape
     rows = ch_dev * win_dev
     block = 256
-    full = lambda i, sel: (0, 0, 0)
-    return pl.pallas_call(
+    peers = pairs.shape[1] // PAIRS_DEV
+    shapes = [(peers * CAP, win_dev, 2 * (CHUNKS[0][1] - CHUNKS[0][0]))]
+    for lo, hi in CHUNKS[1:]:
+        shapes += [(CAP, win_dev, 2 * (hi - lo))] * peers
+    outs = pl.pallas_call(
         whiten_kernel,
-        out_shape=jax.ShapeDtypeStruct((sel.shape[0], win_dev, 2 * NF), BF16),
+        out_shape=[pltpu.HBM(shape, BF16) for shape in shapes],
         grid_spec=pltpu.PrefetchScalarGridSpec(
             num_scalar_prefetch=1,
             grid=(rows // block,),
             in_specs=[
-                pl.BlockSpec((block, samples), lambda i, sel: (i, 0)),
-                pl.BlockSpec(base.shape, full),
-                pl.BlockSpec(step.shape, full),
+                pl.BlockSpec(pairs.shape, lambda i, owner: (0, 0)),
+                pl.BlockSpec((block, samples), lambda i, owner: (i, 0)),
+                pl.BlockSpec(parts.shape, lambda i, owner: (0, 0, 0)),
             ],
-            out_specs=pl.BlockSpec((sel.shape[0], win_dev, 2 * NF), full),
-            scratch_shapes=[
+            out_specs=[pl.BlockSpec(memory_space=pltpu.HBM)] * len(shapes),
+            scratch_shapes=[pltpu.VMEM(shape, BF16) for shape in shapes]
+            + [
                 pltpu.VMEM((samples, 2 * NF), BF16),
                 pltpu.VMEM((ch_dev, win_dev, 2 * NF), BF16),
+                pltpu.VMEM((CAP, PAIRS_DEV), jnp.int32),
+                pltpu.SMEM((CAP, PAIRS_DEV), jnp.int32),
+                pltpu.SemaphoreType.DMA,
+                pltpu.SemaphoreType.DMA((len(shapes),)),
             ],
         ),
         compiler_params=pltpu.CompilerParams(
-            dimension_semantics=("arbitrary",), vmem_limit_bytes=48 << 20
+            dimension_semantics=("arbitrary",), vmem_limit_bytes=24 << 20
         ),
         name="whiten",
-    )(sel, records.reshape(rows, samples), base, step)
+    )(owner, *map(in_hbm, (pairs, records.reshape(rows, samples), parts)))
+    return outs[0], [outs[1 + j * peers : 1 + (j + 1) * peers] for j in range(len(CHUNKS) - 1)]
 
 
 def inverse_kernel(sketch_ref, base_ref, step_ref, inv_ref, s3_ref):
@@ -182,49 +245,83 @@
             jax.ShapeDtypeStruct((2 * NF, LAGS), BF16),
             jax.ShapeDtypeStruct((3 * RANK, 2 * NF), BF16),
         ),
-        compiler_params=pltpu.CompilerParams(vmem_limit_bytes=32 << 20),
+        compiler_params=pltpu.CompilerParams(vmem_limit_bytes=12 << 20),
         name="inverse_table",
     )(sketch, base, step)
 
 
-def cross_kernel(slot_ref, arr_ref, out_ref):
+def cross_kernel(slot_ref, *rest):
+    if len(rest) == 2:
+        arr, out_ref = rest
+    else:
+        blocks, (out_ref, arr) = rest[:-2], rest[-2:]
+
+        @pl.when(pl.program_id(0) == 0)
+        def _():
+            size = blocks[0].shape[0]
+            for n, block in enumerate(blocks):
+                arr[n * size : (n + 1) * size] = block[...]
+
     i = pl.program_id(0)
-    group = out_ref.shape[1]
-    for q in range(group):
-        left = arr_ref[slot_ref[0, i * group + q]].astype(F32)
-        right = arr_ref[slot_ref[1, i * group + q]].astype(F32)
-        lre, lim = left[:, :NF], left[:, NF:]
-        rre, rim = right[:, :NF], right[:, NF:]
-        out_ref[0, q, :, :NF] = (lre * rre + lim * rim).astype(BF16)
-        out_ref[0, q, :, NF:] = (lim * rre - lre * rim).astype(BF16)
-
-
-def correlate(slots, arrived, parts):
-    windows = arrived.shape[1]
+    some, group = out_ref.shape[:2]
+    bins = out_ref.shape[3] // 2
+
+    def body(n, carry):
+        at = (i * some + n) * group
+        for q in range(group):
+            left = arr[slot_ref[0, at + q]].astype(F32)
+            right = arr[slot_ref[1, at + q]].astype(F32)
+            lre, lim = left[:, :bins], left[:, bins:]
+            rre, rim = right[:, :bins], right[:, bins:]
+            out_ref[n, q, :, :bins] = (lre * rre + lim * rim).astype(BF16)
+            out_ref[n, q, :, bins:] = (lim * rre - lre * rim).astype(BF16)
+        return carry
+
+    lax.fori_loop(0, some, body, 0)
+
+
+def correlate(slots, blocks, parts):
+    size, windows, width = blocks[0].shape
     group = PAIRS_DEV // parts
+    some = 4 if parts % 4 == 0 else 1
+    scratch = []
+    if len(blocks) > 1:
+        scratch = [pltpu.VMEM((size * len(blocks), windows, width), BF16)]
     return pl.pallas_call(
         cross_kernel,
-        out_shape=jax.ShapeDtypeStruct((parts, group, windows, 2 * NF), BF16),
+        out_shape=jax.ShapeDtypeStruct((parts, group, windows, width), BF16),
         grid_spec=pltpu.PrefetchScalarGridSpec(
             num_scalar_prefetch=1,
-            grid=(parts,),
-            in_specs=[pl.BlockSpec(arrived.shape, lambda i, s: (0, 0, 0))],
-            out_specs=pl.BlockSpec((1, group, windows, 2 * NF), lambda i, s: (i, 0, 0, 0)),
+            grid=(parts // some,),
+            in_specs=[pl.BlockSpec(blocks[0].shape, lambda i, s: (0, 0, 0))] * len(blocks),
+            out_specs=pl.BlockSpec((some, group, windows, width), lambda i, s: (i, 0, 0, 0)),
+            scratch_shapes=scratch,
         ),
         compiler_params=pltpu.CompilerParams(
-            dimension_semantics=("arbitrary",), vmem_limit_bytes=32 << 20
+            dimension_semantics=("arbitrary",), vmem_limit_bytes=12 << 20
         ),
         name="cross",
-    )(slots, arrived)
-
-
-def stack_kernel(c_ref, s3_ref, e_ref, o_ref, r_s, h_s, y_s, g_s, en_s):
-    parts, group, windows, width = c_ref.shape
+    )(slots, *blocks)
+
+
+def stack_kernel(*refs):
+    c_refs, refs = refs[: len(CHUNKS)], refs[len(CHUNKS) :]
+    s3_ref, e_ref, o_ref, r_s, h_s, y_s, g_s, en_s = refs
+    parts, group, windows, _ = c_refs[0].shape
+    width = 2 * NF
     count = parts * windows
     s3 = s3_ref[...]
+
+    def pair(p):
+        pieces = [c_ref[:, p].reshape(count, c_ref.shape[3]) for c_ref in c_refs]
+        halves = [piece.shape[1] // 2 for piece in pieces]
+        real = [piece[:, :n] for piece, n in zip(pieces, halves)]
+        imag = [piece[:, n:] for piece, n in zip(pieces, halves)]
+        return jnp.concatenate(real + imag, axis=1)
+
     probes = []
     for p in range(group):
-        c = c_ref[:, p].reshape(count, width)
+        c = pair(p)
         probe = sum3(dot_nt(s3, c))
         probes.append(probe)
         r_s[:, p, :] = sum3(dot_nn(split3(probe), c))
@@ -242,7 +339,7 @@
     row = lax.broadcasted_iota(jnp.int32, (RANK, 128), 0)
     unit = (lane == row + RANK).astype(F32)
     for p in range(group):
-        c = c_ref[:, p].reshape(count, width)
+        c = pair(p)
         y = sum3(dot_nt(split3(h_s[:, p, :]), c))
         gram = dot_nt(y, probes[p], lax.Precision.HIGHEST)
         y_s[:, p, :] = y
@@ -274,8 +371,9 @@
         o_ref[t] = stack
 
 
-def stack_up(cross, s3, excess):
-    parts, group, windows, width = cross.shape
+def stack_up(crosses, s3, excess):
+    parts, group, windows, _ = crosses[0].shape
+    width = 2 * NF
     return pl.pallas_call(
         stack_kernel,
         out_shape=jax.ShapeDtypeStruct((parts, group, width), F32),
@@ -286,9 +384,9 @@
             pltpu.VMEM((RANK, group, 128), F32),
             pltpu.VMEM((group, width), F32),
         ],
-        compiler_params=pltpu.CompilerParams(vmem_limit_bytes=48 << 20),
+        compiler_params=pltpu.CompilerParams(vmem_limit_bytes=24 << 20),
         name="stack",
-    )(cross, s3, excess)
+    )(*crosses, s3, excess)
 
 
 def lags_kernel(x_ref, inv_ref, o_ref, x2):
@@ -316,7 +414,7 @@
         out_specs=pl.BlockSpec((rows, block), lambda i: (0, i)),
         scratch_shapes=[pltpu.VMEM((2 * rows, width), BF16)],
         compiler_params=pltpu.CompilerParams(
-            dimension_semantics=("arbitrary",), vmem_limit_bytes=32 << 20
+            dimension_semantics=("arbitrary",), vmem_limit_bytes=12 << 20
         ),
         name="lags",
     )(x, inverse)
@@ -329,30 +427,38 @@
     owner = lax.axis_index("pair")
     ch_dev, win_dev, _ = records.shape
 
-    wanted = pair_list.reshape(n_pair, 2 * PAIRS_DEV) - owner * ch_dev
-    column = jnp.arange(ch_dev)
-    asked = jnp.any(wanted[:, :, None] == column[None, None, :], axis=1)
-    before = jnp.sum(asked[:, :, None] & (column[:, None] < column[None, :]), axis=1)
-    slot = jnp.arange(CAP)
-    picked = asked[:, None, :] & (before[:, None, :] == slot[None, :, None])
-    sel = jnp.sum(jnp.where(picked, column, 0), axis=2).astype(jnp.int32).reshape(-1)
-    outgoing = whiten(records, sel, base, step)
-
-    mine = lax.dynamic_slice_in_dim(pair_list, owner * PAIRS_DEV, PAIRS_DEV, 0).T
+    pairs = pair_list.T
+    parts = np.concatenate([base, step])
+    out_first, out_rest = whiten(records, pairs, owner.astype(jnp.int32).reshape(1), parts)
+
+    mine = lax.dynamic_slice_in_dim(pairs, owner * PAIRS_DEV, PAIRS_DEV, 1)
     everyone = jnp.arange(n_pair * ch_dev)
     held = jnp.any(mine.reshape(-1)[:, None] == everyone[None, :], axis=0)
     block = mine // ch_dev
     first = (block * ch_dev)[:, :, None]
     ahead = held & (everyone >= first) & (everyone < mine[:, :, None])
-    slots = (block * CAP + jnp.sum(ahead, axis=2)).astype(jnp.int32)
-
-    arrived = lax.all_to_all(
-        outgoing.reshape(n_pair, CAP, win_dev, 2 * NF), "pair", 0, 0, tiled=True
-    ).reshape(n_pair * CAP, win_dev, 2 * NF)
+    rank = jnp.sum(ahead, axis=2)
+    slots = (block * CAP + rank).astype(jnp.int32)
+    slots_rest = ((block ^ owner) * CAP + rank).astype(jnp.int32)
+
+    shape = (n_pair, CAP) + out_first.shape[1:]
+    arrived = lax.all_to_all(out_first.reshape(shape), "pair", 0, 0, tiled=True)
     inverse, s3 = inverse_table(sketch, ibase, istep)
-    cross = correlate(slots, arrived, n_tm)
-    cross = lax.all_to_all(cross, "tm", 0, 0, tiled=True)
-    stack = stack_up(cross, s3, gram_excess())
+    blocks = [arrived.reshape(out_first.shape)]
+    blocks, out_rest, inverse, s3 = lax.optimization_barrier((blocks, out_rest, inverse, s3))
+    crosses = []
+    for j in range(len(CHUNKS)):
+        cross = correlate(slots_rest if j else slots, blocks, n_tm)
+        crosses.append(lax.all_to_all(cross, "tm", 0, 0, tiled=True))
+        if j + 1 < len(CHUNKS):
+            sent = out_rest[j]
+            if j:
+                blocks, sent = lax.optimization_barrier((blocks, sent))
+            blocks = [sent[0]] + [
+                lax.ppermute(sent[x], "pair", [(o, o ^ x) for o in range(n_pair)])
+                for x in range(1, n_pair)
+            ]
+    stack = stack_up(crosses, s3, gram_excess())
     stack = lax.all_to_all(stack, "tm", 0, 0, tiled=True)
     return to_lags(stack.reshape(PAIRS_DEV, 2 * NF), inverse)
 

time: 164 us -> 141 us (0.86)
  waiting for transfers between devices: 94.3 us -> 37.7 us
  blocking collectives: 14.6 us -> 46.7 us
  starting transfers between devices: 12.6 us -> 19.4 us
  local copies, waits for them, and re-layouts: 8.73 us -> 2.67 us
  Pallas kernels: 30.3 us -> 32.9 us
    all_to_all x2, waiting for transfers between devices: 94.3 us -> 18.5 us  [the longest x1 14.8 us: local(): arrived = lax.all_to_all(out_first.reshape(shape), 'pair', 0, 0, tiled=True)]
    all_to_all x0 -> x1, blocking collectives: none -> 32.6 us  [local(): crosses.append(lax.all_to_all(cross, 'tm', 0, 0, tiled=True))]
    ppermute x0 -> x7, waiting for transfers between devices: none -> 19.1 us  [local(): lax.ppermute(sent[x], 'pair', [(o, o ^ x) for o in range(n_pair)])]
    ppermute x0 -> x7, starting transfers between devices: none -> 6.64 us  [local(): lax.ppermute(sent[x], 'pair', [(o, o ^ x) for o in range(n_pair)])]
    unnamed x20 -> x28, local copies, waits for them, and re-layouts: 7.39 us -> 1.99 us
    pallas_call x1 -> x2, Pallas kernels: 2.3 us -> 4.49 us  [correlate(): pl.pallas_call(cross_kernel, out_shape=jax.ShapeDtypeStruct((parts, group...]
  transfers between devices with their start and end apart: 2 -> 9, of which waited for: 2 -> 8; matrix products, arithmetic and copies ran while one was open for 1% -> 1% of each run, Pallas kernels for 2% -> 3%
where the time goes in v2:
time: 141 us
  blocking collectives  46.7 us (33%)
  waiting for transfers between devices  37.7 us (27%)
  Pallas kernels  32.9 us (23%)
  starting transfers between devices  19.4 us (14%)
  local copies, waits for them, and re-layouts  2.67 us (2%)
    all_to_all x1, blocking collectives, local(): crosses.append(lax.all_to_all(cross, 'tm', 0, 0, tiled=True))  32.6 us
    ppermute x7, waiting for transfers between devices, local(): lax.ppermute(sent[x], 'pair', [(o, o ^ x) for o in range(n_pair)])  19.1 us
    all_to_all x1, waiting for transfers between devices, local(): arrived = lax.all_to_all(out_first.reshape(shape), 'pair', 0, 0, tiled=True)  14.8 us
    all_to_all x1, blocking collectives, local(): stack = lax.all_to_all(stack, 'tm', 0, 0, tiled=True)  14 us
    pallas_call x1, Pallas kernels, stack_up(): pl.pallas_call(stack_kernel, out_shape=jax.ShapeDtypeStruct((parts, group...  12.2 us
    pallas_call x1, Pallas kernels, whiten(): pl.pallas_call(whiten_kernel, out_shape=[pltpu.HBM(shape, BF16) for shape...  10.1 us
    all_to_all x1, starting transfers between devices, local(): crosses.append(lax.all_to_all(cross, 'tm', 0, 0, tiled=True))  7.23 us
    ppermute x7, starting transfers between devices, local(): lax.ppermute(sent[x], 'pair', [(o, o ^ x) for o in range(n_pair)])  6.64 us
  transfers between devices with their start and end apart: 9, of which 8 were waited for; matrix products, arithmetic and copies ran while one was open for 1% of the time, Pallas kernels for 3%

profile of v2, /device:TPU:0, one launch (start us, length us, event | category | flops | bytes accessed | tf_op | source)
XLA Modules:
  0.0 140.6 jit_solution(10108030431982268633)
XLA Ops:
  0.0 10.1 %whiten.1 = (bf16[96,16,512]{2,1,0:T(8,128)(2,1)}, bf16[12,16,512]{2,1,0:T(8,128)(2,1)}, bf16[12,16,512]{2,1,0:T(8,128)(2,1)}, bf16[12,16,512]{2,1,0:T(8,128)(2,...) custom-call(s32[1]{0:T(128)} %bitcast.2.owner_ref, ...), custom_call_target="tpu_custom_call" | custom-call | tf_op jit(solution)/shard_map/whiten/pallas_call | solution.py:192
  10.1 0.0 copy-start.3
  10.1 0.0 copy-start.4
  10.2 5.5 %all-to-all-start = ((bf16[8,12,16,512]{3,2,1,0:T(8,128)(2,1)}), bf16[8,12,16,512]{3,2,1,0:T(8,128)(2,1)S(1)}, u32[]{:S(2)}, u32[]{:S(2)}) async-start(bf16[8,12,16,512]{3,2,1,0:T(8,128)(2,1)} %bitcast.15), calls=%async_computation | async-start | bytes 3145728 | tf_op jit(solution)/shard_map/all_to_all | solution.py:445
  15.7 3.0 %inverse_table.1 = (bf16[1024,2048]{1,0:T(8,128)(2,1)S(1)}, bf16[48,1024]{1,0:T(8,128)(2,1)S(1)}) custom-call(f32[16,2048]{1,0:T(8,128)S(1)} %copy-done.6, f32[2,32,2048]{2,1,0:T(8,128)S(1)} %copy-done.3, f32[2,16,2048]{2,1,0:T(8,128)S(1)} %copy-done.4), custom_call_target="tpu_custom_call" | custom-call | tf_op jit(solution)/shard_map/inverse_table/pallas_call | solution.py:242
  18.8 1.9 %copy-done = bf16[1024,2048]{1,0:T(8,128)(2,1)} copy-done((bf16[1024,2048]{1,0:T(8,128)(2,1)}, bf16[1024,2048]{1,0:T(8,128)(2,1)S(1)}, u32[]{:S(2)}) %copy-start) | copy-done | bytes 4194328
  20.7 0.7 dynamic-slice_bitcast_fusion
  21.4 0.7 broadcast_multiply_fusion
  22.0 0.1 fusion
  22.2 0.3 convert_reduce_fusion
  22.5 14.8 %all-to-all-done = bf16[8,12,16,512]{3,2,1,0:T(8,128)(2,1)S(1)} async-done(((bf16[8,12,16,512]{3,2,1,0:T(8,128)(2,1)}), bf16[8,12,16,512]{3,2,1,0:T(8,128)(2,1)S(1)}, u32[]{:S(2)}, u32[]{:S(2)}) %all-to-all-start) | async-done | bytes 1572896 | tf_op jit(solution)/shard_map/all_to_all | solution.py:445
  37.3 2.9 %cross.2 = bf16[16,8,16,512]{3,2,1,0:T(8,128)(2,1)} custom-call(s32[2,128]{1,0:T(2,128)S(1)} %get-tuple-element.53.slot_ref, bf16[96,16,512]{2,1,0:T(8,128)(2,1)S(1)} %bitcast.12), custom_call_target="tpu_custom_call" | custom-call | tf_op jit(solution)/shard_map/cross/pallas_call | solution.py:290
  40.2 7.2 %all-to-all-start.1 = ((bf16[16,8,16,512]{3,2,1,0:T(8,128)(2,1)}), bf16[16,8,16,512]{3,2,1,0:T(8,128)(2,1)}, u32[]{:S(2)}, u32[]{:S(2)}) async-start(bf16[16,8,16,512]{3,2,1,0:T(8,128)(2,1)} %cross.2), calls=%async_computation.1 | async-start | bytes 4194304 | tf_op jit(solution)/shard_map/all_to_all | solution.py:452
  47.5 0.1 collective-permute-start
  47.6 0.6 collective-permute-start.1
  48.2 1.2 collective-permute-start.2
  49.4 0.9 collective-permute-start.3
  50.4 2.3 %collective-permute-start.4 = (bf16[12,16,512]{2,1,0:T(8,128)(2,1)S(1)}, bf16[12,16,512]{2,1,0:T(8,128)(2,1)S(1)}, u32[]{:S(2)}, u32[]{:S(2)}) collective-permute-start(bf16[12,16,512]{2,1,0:T(8,128)(2,1)S(1)} %copy-done.9), channel_id=1, source_target_pairs={{0,80},{16,64},{32,112},{48,96},{64,16},{80,0},{96,48},{112,32},{1... | collective-permute-start | bytes 589832 | tf_op jit(solution)/shard_map/ppermute | solution.py:458
  52.7 1.2 collective-permute-start.5
  53.8 1.5 %collective-permute-done.1.rest_2_ = bf16[12,16,512]{2,1,0:T(8,128)(2,1)S(1)} collective-permute-done((bf16[12,16,512]{2,1,0:T(8,128)(2,1)S(1)}, bf16[12,16,512]{2,1,0:T(8,128)(2,1)S(1)}, u32[]{:S(2)}, u32[]{:S(2)}) %collective-permute-start.1) | collective-permute-done | bytes 196640 | tf_op jit(solution)/shard_map/ppermute | solution.py:458
  55.4 0.3 collective-permute-start.6
  55.7 2.9 %collective-permute-done.2.rest_3_ = bf16[12,16,512]{2,1,0:T(8,128)(2,1)S(1)} collective-permute-done((bf16[12,16,512]{2,1,0:T(8,128)(2,1)S(1)}, bf16[12,16,512]{2,1,0:T(8,128)(2,1)S(1)}, u32[]{:S(2)}, u32[]{:S(2)}) %collective-permute-start.2) | collective-permute-done | bytes 196640 | tf_op jit(solution)/shard_map/ppermute | solution.py:458
  58.6 5.9 %collective-permute-done.3.rest_4_ = bf16[12,16,512]{2,1,0:T(8,128)(2,1)S(1)} collective-permute-done((bf16[12,16,512]{2,1,0:T(8,128)(2,1)S(1)}, bf16[12,16,512]{2,1,0:T(8,128)(2,1)S(1)}, u32[]{:S(2)}, u32[]{:S(2)}) %collective-permute-start.3) | collective-permute-done | bytes 196640 | tf_op jit(solution)/shard_map/ppermute | solution.py:458
  64.5 3.3 %collective-permute-done.4.rest_5_ = bf16[12,16,512]{2,1,0:T(8,128)(2,1)S(1)} collective-permute-done((bf16[12,16,512]{2,1,0:T(8,128)(2,1)S(1)}, bf16[12,16,512]{2,1,0:T(8,128)(2,1)S(1)}, u32[]{:S(2)}, u32[]{:S(2)}) %collective-permute-start.4) | collective-permute-done | bytes 196640 | tf_op jit(solution)/shard_map/ppermute | solution.py:458
  67.8 2.3 %collective-permute-done.5.rest_6_ = bf16[12,16,512]{2,1,0:T(8,128)(2,1)S(1)} collective-permute-done((bf16[12,16,512]{2,1,0:T(8,128)(2,1)S(1)}, bf16[12,16,512]{2,1,0:T(8,128)(2,1)S(1)}, u32[]{:S(2)}, u32[]{:S(2)}) %collective-permute-start.5) | collective-permute-done | bytes 196640 | tf_op jit(solution)/shard_map/ppermute | solution.py:458
  70.0 3.3 %collective-permute-done.6.rest_7_ = bf16[12,16,512]{2,1,0:T(8,128)(2,1)S(1)} collective-permute-done((bf16[12,16,512]{2,1,0:T(8,128)(2,1)S(1)}, bf16[12,16,512]{2,1,0:T(8,128)(2,1)S(1)}, u32[]{:S(2)}, u32[]{:S(2)}) %collective-permute-start.6) | collective-permute-done | bytes 196640 | tf_op jit(solution)/shard_map/ppermute | solution.py:458
  73.3 1.6 %cross.3 = bf16[16,8,16,512]{3,2,1,0:T(8,128)(2,1)S(1)} custom-call(s32[2,128]{1,0:T(2,128)S(1)} %get-tuple-element.52.slot_ref, bf16[12,16,512]{2,1,0:T(8,128)(2,1)S(1)} %copy-done.5, bf16[12,16,512]{2,1,0:T(8,128)(2,1)S(1)} %collective-permute-done.rest_1_, bf16[12,16,512]{2,1,0:T(8,128)(2,1)S(1)} %collective-permute-done.1.rest_2_, ...), custom_call_target="tpu_custom_call" | custom-call | tf_op jit(solution)/shard_map/cross/pallas_call | solution.py:290
  74.9 3.7 %all-to-all-done.1.refs_0_ = bf16[16,8,16,512]{3,2,1,0:T(8,128)(2,1)} async-done(((bf16[16,8,16,512]{3,2,1,0:T(8,128)(2,1)}), bf16[16,8,16,512]{3,2,1,0:T(8,128)(2,1)}, u32[]{:S(2)}, u32[]{:S(2)}) %all-to-all-start.1) | async-done | bytes 2097184 | tf_op jit(solution)/shard_map/all_to_all | solution.py:452
  78.6 32.6 %all_to_all.20.refs_1_ = bf16[16,8,16,512]{3,2,1,0:T(8,128)(2,1)S(1)} all-to-all(bf16[16,8,16,512]{3,2,1,0:T(8,128)(2,1)S(1)} %cross.3), channel_id=1, replica_groups=mesh['pair'=8,'tm'=16] {'tm'}, dimensions={0} | all-to-all | bytes 4194304 | tf_op jit(solution)/shard_map/all_to_all | solution.py:452
  111.3 12.2 %stack.1 = f32[16,8,1024]{2,1,0:T(8,128)S(1)} custom-call(bf16[16,8,16,512]{3,2,1,0:T(8,128)(2,1)} %all-to-all-done.1.refs_0_, bf16[16,8,16,512]{3,2,1,0:T(8,128)(2,1)S(1)} %all_to_all.20.refs_1_, bf16[48,1024]{1,0:T(8,128)(2,1)S(1)} %get-tuple-element.47.refs_2_, bf16[2,512,512]{2,1,0:T(8,128)(2,1)S(1)} %copy-done.2), custom_call_target="tpu_custom_call" | custom-call | tf_op jit(solution)/shard_map/stack/pallas_call | solution.py:377
  123.5 14.0 %all_to_all.21 = f32[16,8,1024]{2,1,0:T(8,128)S(1)} all-to-all(f32[16,8,1024]{2,1,0:T(8,128)S(1)} %stack.1), channel_id=1, replica_groups=mesh['pair'=8,'tm'=16] {'tm'}, dimensions={0} | all-to-all | bytes 1048576 | tf_op jit(solution)/shard_map/all_to_all | solution.py:462
  137.5 3.1 %lags.1 = f32[128,2048]{1,0:T(8,128)} custom-call(f32[128,1024]{1,0:T(8,128)S(1)} %bitcast.13, bf16[1024,2048]{1,0:T(8,128)(2,1)S(1)} %copy-done.1), custom_call_target="tpu_custom_call" | custom-call | tf_op jit(solution)/shard_map/lags/pallas_call | solution.py:406
  (27 shorter events, 0.1 us)
Async XLA Ops:
  10.1 5.6 %copy-start.3 = (f32[2,32,2048]{2,1,0:T(8,128)S(1)}, f32[2,32,2048]{2,1,0:T(8,128)}, u32[]{:S(2)}) copy-start(f32[2,32,2048]{2,1,0:T(8,128)} %constant.42.clone.base_ref) | copy-start | bytes 1572868
  10.1 5.6 %copy-start.4 = (f32[2,16,2048]{2,1,0:T(8,128)S(1)}, f32[2,16,2048]{2,1,0:T(8,128)}, u32[]{:S(2)}) copy-start(f32[2,16,2048]{2,1,0:T(8,128)} %constant.43.clone.step_ref) | copy-start | bytes 786436
  10.2 5.6 %copy-start.6 = (f32[16,2048]{1,0:T(8,128)S(1)}, f32[16,2048]{1,0:T(8,128)}, u32[]{:S(2)}) copy-start(f32[16,2048]{1,0:T(8,128)} %sketch_ref.1) | copy-start | bytes 393220
  10.2 27.1 %all-to-all-start = ((bf16[8,12,16,512]{3,2,1,0:T(8,128)(2,1)}), bf16[8,12,16,512]{3,2,1,0:T(8,128)(2,1)S(1)}, u32[]{:S(2)}, u32[]{:S(2)}) async-start(bf16[8,12,16,512]{3,2,1,0:T(8,128)(2,1)} %bitcast.15), calls=%async_computation | async-start | bytes 3145728 | tf_op jit(solution)/shard_map/all_to_all | solution.py:445
  18.7 1.9 %copy-start = (bf16[1024,2048]{1,0:T(8,128)(2,1)}, bf16[1024,2048]{1,0:T(8,128)(2,1)S(1)}, u32[]{:S(2)}) copy-start(bf16[1024,2048]{1,0:T(8,128)(2,1)S(1)} %get-tuple-element.48.inv_ref) | copy-start | bytes 12582916
  40.2 7.3 %copy-start.13 = (bf16[12,16,512]{2,1,0:T(8,128)(2,1)S(1)}, bf16[12,16,512]{2,1,0:T(8,128)(2,1)}, u32[]{:S(2)}) copy-start(bf16[12,16,512]{2,1,0:T(8,128)(2,1)} %get-tuple-element.40) | copy-start | bytes 589828
  40.2 7.4 %copy-start.12 = (bf16[12,16,512]{2,1,0:T(8,128)(2,1)S(1)}, bf16[12,16,512]{2,1,0:T(8,128)(2,1)}, u32[]{:S(2)}) copy-start(bf16[12,16,512]{2,1,0:T(8,128)(2,1)} %get-tuple-element.41) | copy-start | bytes 589828
  40.2 8.0 %copy-start.11 = (bf16[12,16,512]{2,1,0:T(8,128)(2,1)S(1)}, bf16[12,16,512]{2,1,0:T(8,128)(2,1)}, u32[]{:S(2)}) copy-start(bf16[12,16,512]{2,1,0:T(8,128)(2,1)} %get-tuple-element.42) | copy-start | bytes 589828
  40.2 9.3 %copy-start.10 = (bf16[12,16,512]{2,1,0:T(8,128)(2,1)S(1)}, bf16[12,16,512]{2,1,0:T(8,128)(2,1)}, u32[]{:S(2)}) copy-start(bf16[12,16,512]{2,1,0:T(8,128)(2,1)} %get-tuple-element.43) | copy-start | bytes 589828
  40.2 10.2 %copy-start.9 = (bf16[12,16,512]{2,1,0:T(8,128)(2,1)S(1)}, bf16[12,16,512]{2,1,0:T(8,128)(2,1)}, u32[]{:S(2)}) copy-start(bf16[12,16,512]{2,1,0:T(8,128)(2,1)} %get-tuple-element.44) | copy-start | bytes 589828
  40.2 12.5 %copy-start.8 = (bf16[12,16,512]{2,1,0:T(8,128)(2,1)S(1)}, bf16[12,16,512]{2,1,0:T(8,128)(2,1)}, u32[]{:S(2)}) copy-start(bf16[12,16,512]{2,1,0:T(8,128)(2,1)} %get-tuple-element.45) | copy-start | bytes 589828
  40.2 15.2 %copy-start.7 = (bf16[12,16,512]{2,1,0:T(8,128)(2,1)S(1)}, bf16[12,16,512]{2,1,0:T(8,128)(2,1)}, u32[]{:S(2)}) copy-start(bf16[12,16,512]{2,1,0:T(8,128)(2,1)} %get-tuple-element.46) | copy-start | bytes 589828
  40.2 33.1 %copy-start.5 = (bf16[12,16,512]{2,1,0:T(8,128)(2,1)S(1)}, bf16[12,16,512]{2,1,0:T(8,128)(2,1)}, u32[]{:S(2)}) copy-start(bf16[12,16,512]{2,1,0:T(8,128)(2,1)} %get-tuple-element.39.rest_0_) | copy-start | bytes 589828
  40.2 38.4 %all-to-all-start.1 = ((bf16[16,8,16,512]{3,2,1,0:T(8,128)(2,1)}), bf16[16,8,16,512]{3,2,1,0:T(8,128)(2,1)}, u32[]{:S(2)}, u32[]{:S(2)}) async-start(bf16[16,8,16,512]{3,2,1,0:T(8,128)(2,1)} %cross.2), calls=%async_computation.1 | async-start | bytes 4194304 | tf_op jit(solution)/shard_map/all_to_all | solution.py:452
  47.5 5.2 %collective-permute-start = (bf16[12,16,512]{2,1,0:T(8,128)(2,1)S(1)}, bf16[12,16,512]{2,1,0:T(8,128)(2,1)S(1)}, u32[]{:S(2)}, u32[]{:S(2)}) collective-permute-start(bf16[12,16,512]{2,1,0:T(8,128)(2,1)S(1)} %copy-done.13), channel_id=1, source_target_pairs={{0,16},{16,0},{32,48},{48,32},{64,80},{80,64},{96,112},{112,96},{1... | collective-permute-start | bytes 589832 | tf_op jit(solution)/shard_map/ppermute | solution.py:458
  47.6 7.8 %collective-permute-start.1 = (bf16[12,16,512]{2,1,0:T(8,128)(2,1)S(1)}, bf16[12,16,512]{2,1,0:T(8,128)(2,1)S(1)}, u32[]{:S(2)}, u32[]{:S(2)}) collective-permute-start(bf16[12,16,512]{2,1,0:T(8,128)(2,1)S(1)} %copy-done.12), channel_id=1, source_target_pairs={{0,32},{16,48},{32,0},{48,16},{64,96},{80,112},{96,64},{112,80},{1... | collective-permute-start | bytes 589832 | tf_op jit(solution)/shard_map/ppermute | solution.py:458
  48.2 10.4 %collective-permute-start.2 = (bf16[12,16,512]{2,1,0:T(8,128)(2,1)S(1)}, bf16[12,16,512]{2,1,0:T(8,128)(2,1)S(1)}, u32[]{:S(2)}, u32[]{:S(2)}) collective-permute-start(bf16[12,16,512]{2,1,0:T(8,128)(2,1)S(1)} %copy-done.11), channel_id=1, source_target_pairs={{0,48},{16,32},{32,16},{48,0},{64,112},{80,96},{96,80},{112,64},{1... | collective-permute-start | bytes 589832 | tf_op jit(solution)/shard_map/ppermute | solution.py:458
  49.4 15.1 %collective-permute-start.3 = (bf16[12,16,512]{2,1,0:T(8,128)(2,1)S(1)}, bf16[12,16,512]{2,1,0:T(8,128)(2,1)S(1)}, u32[]{:S(2)}, u32[]{:S(2)}) collective-permute-start(bf16[12,16,512]{2,1,0:T(8,128)(2,1)S(1)} %copy-done.10), channel_id=1, source_target_pairs={{0,64},{16,80},{32,96},{48,112},{64,0},{80,16},{96,32},{112,48},{1... | collective-permute-start | bytes 589832 | tf_op jit(solution)/shard_map/ppermute | solution.py:458
  50.4 17.4 %collective-permute-start.4 = (bf16[12,16,512]{2,1,0:T(8,128)(2,1)S(1)}, bf16[12,16,512]{2,1,0:T(8,128)(2,1)S(1)}, u32[]{:S(2)}, u32[]{:S(2)}) collective-permute-start(bf16[12,16,512]{2,1,0:T(8,128)(2,1)S(1)} %copy-done.9), channel_id=1, source_target_pairs={{0,80},{16,64},{32,112},{48,96},{64,16},{80,0},{96,48},{112,32},{1... | collective-permute-start | bytes 589832 | tf_op jit(solution)/shard_map/ppermute | solution.py:458
  52.7 17.3 %collective-permute-start.5 = (bf16[12,16,512]{2,1,0:T(8,128)(2,1)S(1)}, bf16[12,16,512]{2,1,0:T(8,128)(2,1)S(1)}, u32[]{:S(2)}, u32[]{:S(2)}) collective-permute-start(bf16[12,16,512]{2,1,0:T(8,128)(2,1)S(1)} %copy-done.8), channel_id=1, source_target_pairs={{0,96},{16,112},{32,64},{48,80},{64,32},{80,48},{96,0},{112,16},{1... | collective-permute-start | bytes 589832 | tf_op jit(solution)/shard_map/ppermute | solution.py:458
  55.4 17.9 %collective-permute-start.6 = (bf16[12,16,512]{2,1,0:T(8,128)(2,1)S(1)}, bf16[12,16,512]{2,1,0:T(8,128)(2,1)S(1)}, u32[]{:S(2)}, u32[]{:S(2)}) collective-permute-start(bf16[12,16,512]{2,1,0:T(8,128)(2,1)S(1)} %copy-done.7), channel_id=1, source_target_pairs={{0,112},{16,96},{32,80},{48,64},{64,48},{80,32},{96,16},{112,0},{1... | collective-permute-start | bytes 589832 | tf_op jit(solution)/shard_map/ppermute | solution.py:458
  74.9 36.3 %copy-start.2 = (bf16[2,512,512]{2,1,0:T(8,128)(2,1)S(1)}, bf16[2,512,512]{2,1,0:T(8,128)(2,1)}, u32[]{:S(2)}) copy-start(bf16[2,512,512]{2,1,0:T(8,128)(2,1)} %constant.44.clone.refs_3_) | copy-start | bytes 3145732
  111.3 26.2 %copy-start.1 = (bf16[1024,2048]{1,0:T(8,128)(2,1)S(1)}, bf16[1024,2048]{1,0:T(8,128)(2,1)}, u32[]{:S(2)}) copy-start(bf16[1024,2048]{1,0:T(8,128)(2,1)} %copy-done) | copy-start | bytes 12582916

commit v3 on v2

--- a/solution.py
+++ b/solution.py
@@ -1,3 +1,4 @@
+import functools
 import math
 
 import jax
@@ -17,7 +18,7 @@
 F0 = NF // 2
 STEP = 32
 ISTEP = 16
-CHUNKS = ((0, 256), (256, 512))
+HALF = 8
 F32 = jnp.float32
 BF16 = jnp.bfloat16
 
@@ -85,10 +86,6 @@
 
 def dot_nn(a, b):
     return jnp.dot(a, b, preferred_element_type=F32)
-
-
-def cut(rows, lo, hi):
-    return jnp.concatenate([rows[:, lo:hi], rows[:, NF + lo : NF + hi]], axis=1)
 
 
 def pick(pair_ref, owner, channels, peers):
@@ -111,12 +108,12 @@
     return jnp.concatenate(rows, axis=0).astype(jnp.int32)
 
 
-def whiten_kernel(owner_ref, pair_ref, rec_ref, parts_ref, *rest):
-    count = 1 + (len(CHUNKS) - 1) * (pair_ref.shape[1] // PAIRS_DEV)
+def whiten_kernel(owner_ref, pair_ref, rec_ref, parts_ref, *rest, swapped):
+    peers = pair_ref.shape[1] // PAIRS_DEV
+    count = peers if swapped else 1
     outs, bufs, rest = rest[:count], rest[count : 2 * count], rest[2 * count :]
     table, white, chosen, sel_ref, chosen_sem, sems = rest
     i = pl.program_id(0)
-    peers = pair_ref.shape[1] // PAIRS_DEV
     owner = owner_ref[0]
     fetch = pltpu.make_async_copy(chosen, sel_ref, chosen_sem)
 
@@ -144,79 +141,74 @@
 
         lax.fori_loop(0, SAMPLES // 2 // STEP, body, 0)
 
-    spectra = dot_nn(rec_ref[...], table[...])
+    per, windows, samples = rec_ref.shape
+    spectra = dot_nn(rec_ref[...].reshape(per * windows, samples), table[...])
     re = spectra[:, :NF]
     im = spectra[:, NF:]
     power = re * re + im * im
     level = jnp.mean(power, axis=1, keepdims=True)
     factor = lax.rsqrt(power + level + 1e-06)
     rows = jnp.concatenate([re * factor, im * factor], axis=1).astype(BF16)
-    channels, windows, width = white.shape
-    per = rec_ref.shape[0] // windows
-    white[pl.ds(i * per, per)] = rows.reshape(per, windows, width)
+    white[pl.ds(i * per, per)] = rows.reshape(per, windows, 2 * NF)
 
     @pl.when(i == pl.num_programs(0) - 1)
     def _():
         fetch.wait()
         sends = []
-
-        def fill(buf, row, peer, lo, hi):
-            def body(n, carry):
-                buf[row + n] = cut(white[sel_ref[n, peer]], lo, hi)
+        for d in range(peers):
+            buf, first = (bufs[d], 0) if swapped else (bufs[0], d * CAP)
+            peer = owner ^ d if swapped else d
+
+            def body(n, carry, buf=buf, first=first, peer=peer):
+                buf[first + n] = white[sel_ref[n, peer]]
                 return carry
 
             lax.fori_loop(0, CAP, body, 0, unroll=4)
-
-        for d in range(peers):
-            fill(bufs[0], d * CAP, d, *CHUNKS[0])
-        sends.append(pltpu.make_async_copy(bufs[0], outs[0], sems.at[0]))
-        sends[-1].start()
-        for j, (lo, hi) in enumerate(CHUNKS[1:]):
-            for x in range(peers):
-                n = 1 + j * peers + x
-                fill(bufs[n], 0, owner ^ x, lo, hi)
-                sends.append(pltpu.make_async_copy(bufs[n], outs[n], sems.at[n]))
-                sends[-1].start()
+            if swapped:
+                sends.append(pltpu.make_async_copy(buf, outs[d], sems.at[d]))
+            else:
+                span = pl.ds(first, CAP)
+                sends.append(pltpu.make_async_copy(buf.at[span], outs[0].at[span], sems.at[d]))
+            sends[-1].start()
         for send in sends:
             send.wait()
 
 
-def whiten(records, pairs, owner, parts):
-    ch_dev, win_dev, samples = records.shape
-    rows = ch_dev * win_dev
-    block = 256
+def whiten(records, pairs, owner, parts, half):
+    ch_dev, _, samples = records.shape
+    block = 32
     peers = pairs.shape[1] // PAIRS_DEV
-    shapes = [(peers * CAP, win_dev, 2 * (CHUNKS[0][1] - CHUNKS[0][0]))]
-    for lo, hi in CHUNKS[1:]:
-        shapes += [(CAP, win_dev, 2 * (hi - lo))] * peers
-    outs = pl.pallas_call(
-        whiten_kernel,
+    if half:
+        shapes = [(CAP, HALF, 2 * NF)] * peers
+    else:
+        shapes = [(peers * CAP, HALF, 2 * NF)]
+    return pl.pallas_call(
+        functools.partial(whiten_kernel, swapped=bool(half)),
         out_shape=[pltpu.HBM(shape, BF16) for shape in shapes],
         grid_spec=pltpu.PrefetchScalarGridSpec(
             num_scalar_prefetch=1,
-            grid=(rows // block,),
+            grid=(ch_dev // block,),
             in_specs=[
                 pl.BlockSpec(pairs.shape, lambda i, owner: (0, 0)),
-                pl.BlockSpec((block, samples), lambda i, owner: (i, 0)),
+                pl.BlockSpec((block, HALF, samples), lambda i, owner: (i, half, 0)),
                 pl.BlockSpec(parts.shape, lambda i, owner: (0, 0, 0)),
             ],
             out_specs=[pl.BlockSpec(memory_space=pltpu.HBM)] * len(shapes),
             scratch_shapes=[pltpu.VMEM(shape, BF16) for shape in shapes]
             + [
                 pltpu.VMEM((samples, 2 * NF), BF16),
-                pltpu.VMEM((ch_dev, win_dev, 2 * NF), BF16),
+                pltpu.VMEM((ch_dev, HALF, 2 * NF), BF16),
                 pltpu.VMEM((CAP, PAIRS_DEV), jnp.int32),
                 pltpu.SMEM((CAP, PAIRS_DEV), jnp.int32),
                 pltpu.SemaphoreType.DMA,
-                pltpu.SemaphoreType.DMA((len(shapes),)),
+                pltpu.SemaphoreType.DMA((peers,)),
             ],
         ),
         compiler_params=pltpu.CompilerParams(
             dimension_semantics=("arbitrary",), vmem_limit_bytes=24 << 20
         ),
         name="whiten",
-    )(owner, *map(in_hbm, (pairs, records.reshape(rows, samples), parts)))
-    return outs[0], [outs[1 + j * peers : 1 + (j + 1) * peers] for j in range(len(CHUNKS) - 1)]
+    )(owner, *map(in_hbm, (pairs, records, parts)))
 
 
 def inverse_kernel(sketch_ref, base_ref, step_ref, inv_ref, s3_ref):
@@ -235,7 +227,7 @@
         return carry
 
     lax.fori_loop(0, NF // ISTEP, body, 0)
-    s3_ref[...] = split3(sum3(dot_nt(split3(sketch_ref[...]), inv_ref[...])))
+    s3_ref[...] = split3(sum3(dot_nt(split3(sketch_ref[...]), inv_ref[...]))).astype(F32).T.astype(BF16)
 
 
 def inverse_table(sketch, base, step):
@@ -243,7 +235,7 @@
         inverse_kernel,
         out_shape=(
             jax.ShapeDtypeStruct((2 * NF, LAGS), BF16),
-            jax.ShapeDtypeStruct((3 * RANK, 2 * NF), BF16),
+            jax.ShapeDtypeStruct((2 * NF, 3 * RANK), BF16),
         ),
         compiler_params=pltpu.CompilerParams(vmem_limit_bytes=12 << 20),
         name="inverse_table",
@@ -280,7 +272,7 @@
     lax.fori_loop(0, some, body, 0)
 
 
-def correlate(slots, blocks, parts):
+def correlate(slots, blocks, parts, space):
     size, windows, width = blocks[0].shape
     group = PAIRS_DEV // parts
     some = 4 if parts % 4 == 0 else 1
@@ -289,7 +281,7 @@
         scratch = [pltpu.VMEM((size * len(blocks), windows, width), BF16)]
     return pl.pallas_call(
         cross_kernel,
-        out_shape=jax.ShapeDtypeStruct((parts, group, windows, width), BF16),
+        out_shape=space((parts, group, windows, width), BF16),
         grid_spec=pltpu.PrefetchScalarGridSpec(
             num_scalar_prefetch=1,
             grid=(parts // some,),
@@ -304,25 +296,19 @@
     )(slots, *blocks)
 
 
-def stack_kernel(*refs):
-    c_refs, refs = refs[: len(CHUNKS)], refs[len(CHUNKS) :]
-    s3_ref, e_ref, o_ref, r_s, h_s, y_s, g_s, en_s = refs
-    parts, group, windows, _ = c_refs[0].shape
-    width = 2 * NF
-    count = parts * windows
+def gather_pair(c_ref, p):
+    parts, _, windows, width = c_ref.shape
+    return c_ref[:, p].reshape(parts * windows, width)
+
+
+def stack_kernel(ca_ref, cb_ref, s3_ref, e_ref, o_ref, r_s, h_s, y_s, g_s, en_s):
+    parts, group, windows, width = ca_ref.shape
+    count = 2 * parts * windows
     s3 = s3_ref[...]
-
-    def pair(p):
-        pieces = [c_ref[:, p].reshape(count, c_ref.shape[3]) for c_ref in c_refs]
-        halves = [piece.shape[1] // 2 for piece in pieces]
-        real = [piece[:, :n] for piece, n in zip(pieces, halves)]
-        imag = [piece[:, n:] for piece, n in zip(pieces, halves)]
-        return jnp.concatenate(real + imag, axis=1)
-
     probes = []
     for p in range(group):
-        c = pair(p)
-        probe = sum3(dot_nt(s3, c))
+        c = jnp.concatenate([gather_pair(ca_ref, p), gather_pair(cb_ref, p)], axis=0)
+        probe = sum3(dot_nn(c, s3).T)
         probes.append(probe)
         r_s[:, p, :] = sum3(dot_nn(split3(probe), c))
         cf = c.astype(F32)
@@ -339,7 +325,7 @@
     row = lax.broadcasted_iota(jnp.int32, (RANK, 128), 0)
     unit = (lane == row + RANK).astype(F32)
     for p in range(group):
-        c = pair(p)
+        c = jnp.concatenate([gather_pair(ca_ref, p), gather_pair(cb_ref, p)], axis=0)
         y = sum3(dot_nt(split3(h_s[:, p, :]), c))
         gram = dot_nt(y, probes[p], lax.Precision.HIGHEST)
         y_s[:, p, :] = y
@@ -372,15 +358,14 @@
 
 
 def stack_up(crosses, s3, excess):
-    parts, group, windows, _ = crosses[0].shape
-    width = 2 * NF
+    parts, group, windows, width = crosses[0].shape
     return pl.pallas_call(
         stack_kernel,
         out_shape=jax.ShapeDtypeStruct((parts, group, width), F32),
         scratch_shapes=[
             pltpu.VMEM((RANK, group, width), F32),
             pltpu.VMEM((RANK, group, width), F32),
-            pltpu.VMEM((RANK, group, parts * windows), F32),
+            pltpu.VMEM((RANK, group, 2 * parts * windows), F32),
             pltpu.VMEM((RANK, group, 128), F32),
             pltpu.VMEM((group, width), F32),
         ],
@@ -390,13 +375,14 @@
 
 
 def lags_kernel(x_ref, inv_ref, o_ref, x2):
-    rows = x_ref.shape[0]
-
-    @pl.when(pl.program_id(0) == 0)
+    rows, block = o_ref.shape
+    i = pl.program_id(0)
+
+    @pl.when(i == 0)
     def _():
         x2[...] = split2(x_ref[...])
 
-    y = dot_nn(x2[...], inv_ref[...])
+    y = dot_nn(x2[...], inv_ref[:, pl.ds(pl.multiple_of(i * block, block), block)])
     o_ref[...] = y[:rows] + y[rows:]
 
 
@@ -409,7 +395,7 @@
         grid=(LAGS // block,),
         in_specs=[
             pl.BlockSpec((rows, width), lambda i: (0, 0)),
-            pl.BlockSpec((width, block), lambda i: (0, i)),
+            pl.BlockSpec((width, LAGS), lambda i: (0, 0)),
         ],
         out_specs=pl.BlockSpec((rows, block), lambda i: (0, i)),
         scratch_shapes=[pltpu.VMEM((2 * rows, width), BF16)],
@@ -429,7 +415,11 @@
 
     pairs = pair_list.T
     parts = np.concatenate([base, step])
-    out_first, out_rest = whiten(records, pairs, owner.astype(jnp.int32).reshape(1), parts)
+    number = owner.astype(jnp.int32).reshape(1)
+    (sent_a,) = whiten(records, pairs, number, parts, 0)
+    shape = (n_pair, CAP) + sent_a.shape[1:]
+    arrived = lax.all_to_all(sent_a.reshape(shape), "pair", 0, 0, tiled=True)
+    sent_b = whiten(records, pairs, number, parts, 1)
 
     mine = lax.dynamic_slice_in_dim(pairs, owner * PAIRS_DEV, PAIRS_DEV, 1)
     everyone = jnp.arange(n_pair * ch_dev)
@@ -441,24 +431,17 @@
     slots = (block * CAP + rank).astype(jnp.int32)
     slots_rest = ((block ^ owner) * CAP + rank).astype(jnp.int32)
 
-    shape = (n_pair, CAP) + out_first.shape[1:]
-    arrived = lax.all_to_all(out_first.reshape(shape), "pair", 0, 0, tiled=True)
     inverse, s3 = inverse_table(sketch, ibase, istep)
-    blocks = [arrived.reshape(out_first.shape)]
-    blocks, out_rest, inverse, s3 = lax.optimization_barrier((blocks, out_rest, inverse, s3))
-    crosses = []
-    for j in range(len(CHUNKS)):
-        cross = correlate(slots_rest if j else slots, blocks, n_tm)
-        crosses.append(lax.all_to_all(cross, "tm", 0, 0, tiled=True))
-        if j + 1 < len(CHUNKS):
-            sent = out_rest[j]
-            if j:
-                blocks, sent = lax.optimization_barrier((blocks, sent))
-            blocks = [sent[0]] + [
-                lax.ppermute(sent[x], "pair", [(o, o ^ x) for o in range(n_pair)])
-                for x in range(1, n_pair)
-            ]
-    stack = stack_up(crosses, s3, gram_excess())
+    blocks_a = arrived.reshape(sent_a.shape)
+    blocks_a, sent_b, inverse, s3 = lax.optimization_barrier((blocks_a, sent_b, inverse, s3))
+    cross_a = lax.all_to_all(correlate(slots, [blocks_a], n_tm, pltpu.HBM), "tm", 0, 0, tiled=True)
+    blocks_b = [sent_b[0]] + [
+        lax.ppermute(sent_b[x], "pair", [(o, o ^ x) for o in range(n_pair)])
+        for x in range(1, n_pair)
+    ]
+    slots_rest, cross_a = lax.optimization_barrier((slots_rest, cross_a))
+    cross_b = lax.all_to_all(correlate(slots_rest, blocks_b, n_tm, jax.ShapeDtypeStruct), "tm", 0, 0, tiled=True)
+    stack = stack_up((cross_a, cross_b), s3, gram_excess())
     stack = lax.all_to_all(stack, "tm", 0, 0, tiled=True)
     return to_lags(stack.reshape(PAIRS_DEV, 2 * NF), inverse)
 

time: 141 us -> 136 us (0.965)
  waiting for transfers between devices: 37.7 us -> 32.7 us
  Pallas kernels: 32.9 us -> 34.7 us
  blocking collectives: 46.7 us -> 44.9 us
    ppermute x7, waiting for transfers between devices: 19.1 us -> 1.77 us  [local(): lax.ppermute(sent_b[x], 'pair', [(o, o ^ x) for o in range(n_pair)])]
    all_to_all x2, waiting for transfers between devices: 18.5 us -> 30.9 us  [the longest x1 22.9 us: local(): lax.all_to_all(correlate(slots, [blocks_a], n_tm, pltpu.HBM), 'tm', 0, 0,...]
    pallas_call x3 -> x4, Pallas kernels: 14.6 us -> 18.8 us  [the longest x2 13.3 us: whiten(): pl.pallas_call(functools.partial(whiten_kernel, swapped=bool(half)), out_...]
    pallas_call x1, Pallas kernels: 12.2 us -> 9.97 us  [stack_up(): pl.pallas_call(stack_kernel, out_shape=jax.ShapeDtypeStruct((parts, group...]
  transfers between devices with their start and end apart: 9 -> 9, of which waited for: 8 -> 3; matrix products, arithmetic and copies ran while one was open for 1% -> 1% of each run, Pallas kernels for 3% -> 7%
where the time goes in v3:
time: 136 us; the launch traced here: 135 us
  blocking collectives  44.9 us (33%)
  Pallas kernels  34.7 us (26%)
  waiting for transfers between devices  32.7 us (24%)
  starting transfers between devices  19 us (14%)
  local copies, waits for them, and re-layouts  2.67 us (2%)
    all_to_all x1, blocking collectives, local(): lax.all_to_all(correlate(slots_rest, blocks_b, n_tm, jax.ShapeDtypeStruct...  31.5 us
    all_to_all x1, waiting for transfers between devices, local(): lax.all_to_all(correlate(slots, [blocks_a], n_tm, pltpu.HBM), 'tm', 0, 0,...  22.9 us
    all_to_all x1, blocking collectives, local(): stack = lax.all_to_all(stack, 'tm', 0, 0, tiled=True)  13.4 us
    pallas_call x2, Pallas kernels, whiten(): pl.pallas_call(functools.partial(whiten_kernel, swapped=bool(half)), out_...  13.3 us
    pallas_call x1, Pallas kernels, stack_up(): pl.pallas_call(stack_kernel, out_shape=jax.ShapeDtypeStruct((parts, group...  9.97 us
    all_to_all x1, waiting for transfers between devices, local(): arrived = lax.all_to_all(sent_a.reshape(shape), 'pair', 0, 0, tiled=True)  7.96 us
    all_to_all x1, starting transfers between devices, local(): lax.all_to_all(correlate(slots, [blocks_a], n_tm, pltpu.HBM), 'tm', 0, 0,...  7.17 us
    ppermute x7, starting transfers between devices, local(): lax.ppermute(sent_b[x], 'pair', [(o, o ^ x) for o in range(n_pair)])  6.42 us
  transfers between devices with their start and end apart: 9, of which 3 were waited for; matrix products, arithmetic and copies ran while one was open for 1% of the time, Pallas kernels for 7%

profile of v3, /device:TPU:0, one launch (start us, length us, event | category | flops | bytes accessed | tf_op | source)
XLA Modules:
  0.0 135.2 jit_solution(14322527579977037658)
XLA Ops:
  0.0 6.6 %whiten.2 = bf16[96,8,1024]{2,1,0:T(8,128)(2,1)} custom-call(s32[1]{0:T(128)} %bitcast.2.owner_ref, s32[2,1024]{1,0:T(2,128)} %bitcast.14, bf16[64,16,2048]{2,1,0:T(8,128)(2,1)} %rec_ref.3, f32[4,32,512]{2,1,0:T(8,128)} %constant.41.clone.parts_ref), custom_call_target="tpu_custom_call" | custom-call | tf_op jit(solution)/shard_map/whiten/pallas_call | solution.py:185
  6.6 5.4 %all-to-all-start = ((bf16[8,12,8,1024]{3,2,1,0:T(8,128)(2,1)}), bf16[8,12,8,1024]{3,2,1,0:T(8,128)(2,1)S(1)}, u32[]{:S(2)}, u32[]{:S(2)}) async-start(bf16[8,12,8,1024]{3,2,1,0:T(8,128)(2,1)} %bitcast.13), calls=%async_computation | async-start | bytes 3145728 | tf_op jit(solution)/shard_map/all_to_all | solution.py:421
  12.0 0.0 copy-start.4
  12.1 0.0 copy-start.6
  12.1 6.7 %whiten.3 = (bf16[12,8,1024]{2,1,0:T(8,128)(2,1)}, bf16[12,8,1024]{2,1,0:T(8,128)(2,1)}, bf16[12,8,1024]{2,1,0:T(8,128)(2,1)}, bf16[12,8,1024]{2,1,0:T(8,128)(2,...) custom-call(s32[1]{0:T(128)} %bitcast.2.owner_ref, ...), custom_call_target="tpu_custom_call" | custom-call | tf_op jit(solution)/shard_map/whiten/pallas_call | solution.py:185
  18.8 3.1 %inverse_table.1 = (bf16[1024,2048]{1,0:T(8,128)(2,1)S(1)}, bf16[1024,48]{1,0:T(8,128)(2,1)S(1)}) custom-call(f32[16,2048]{1,0:T(8,128)S(1)} %copy-done.6, f32[2,32,2048]{2,1,0:T(8,128)S(1)} %copy-done.3, f32[2,16,2048]{2,1,0:T(8,128)S(1)} %copy-done.4), custom_call_target="tpu_custom_call" | custom-call | tf_op jit(solution)/shard_map/inverse_table/pallas_call | solution.py:234
  21.9 2.0 %copy-done = bf16[1024,2048]{1,0:T(8,128)(2,1)} copy-done((bf16[1024,2048]{1,0:T(8,128)(2,1)}, bf16[1024,2048]{1,0:T(8,128)(2,1)S(1)}, u32[]{:S(2)}) %copy-start) | copy-done | bytes 4194328
  23.9 0.7 dynamic-slice_bitcast_fusion
  24.5 0.7 broadcast_multiply_fusion
  25.2 0.1 fusion
  25.4 0.3 convert_reduce_fusion
  25.7 8.0 %all-to-all-done = bf16[8,12,8,1024]{3,2,1,0:T(8,128)(2,1)S(1)} async-done(((bf16[8,12,8,1024]{3,2,1,0:T(8,128)(2,1)}), bf16[8,12,8,1024]{3,2,1,0:T(8,128)(2,1)S(1)}, u32[]{:S(2)}, u32[]{:S(2)}) %all-to-all-start) | async-done | bytes 1572896 | tf_op jit(solution)/shard_map/all_to_all | solution.py:421
  33.6 2.9 %cross.2 = bf16[16,8,8,1024]{3,2,1,0:T(8,128)(2,1)} custom-call(s32[2,128]{1,0:T(2,128)S(1)} %get-tuple-element.54.slot_ref, bf16[96,8,1024]{2,1,0:T(8,128)(2,1)S(1)} %bitcast.11), custom_call_target="tpu_custom_call" | custom-call | tf_op jit(solution)/shard_map/cross/pallas_call | solution.py:282
  36.5 7.2 %all-to-all-start.1 = ((bf16[16,8,8,1024]{3,2,1,0:T(8,128)(2,1)}), bf16[16,8,8,1024]{3,2,1,0:T(8,128)(2,1)S(1)}, u32[]{:S(2)}, u32[]{:S(2)}) async-start(bf16[16,8,8,1024]{3,2,1,0:T(8,128)(2,1)} %cross.2), calls=%async_computation.1 | async-start | bytes 4194304 | tf_op jit(solution)/shard_map/all_to_all | solution.py:437
  43.7 0.1 collective-permute-start
  43.8 0.6 collective-permute-start.1
  44.4 1.2 collective-permute-start.2
  45.6 0.9 collective-permute-start.3
  46.5 2.3 %collective-permute-start.4 = (bf16[12,8,1024]{2,1,0:T(8,128)(2,1)}, bf16[12,8,1024]{2,1,0:T(8,128)(2,1)S(1)}, u32[]{:S(2)}, u32[]{:S(2)}) collective-permute-start(bf16[12,8,1024]{2,1,0:T(8,128)(2,1)} %get-tuple-element.46), channel_id=1, source_target_pairs={{0,80},{16,64},{32,112},{48,96},{64,16},{80,0},{96,48},{112,32},{1... | collective-permute-start | bytes 589832 | tf_op jit(solution)/shard_map/ppermute | solution.py:439
  48.8 1.2 collective-permute-start.5
  50.0 1.8 %collective-permute-done.1.rest_2_ = bf16[12,8,1024]{2,1,0:T(8,128)(2,1)S(1)} collective-permute-done((bf16[12,8,1024]{2,1,0:T(8,128)(2,1)}, bf16[12,8,1024]{2,1,0:T(8,128)(2,1)S(1)}, u32[]{:S(2)}, u32[]{:S(2)}) %collective-permute-start.1) | collective-permute-done | bytes 196640 | tf_op jit(solution)/shard_map/ppermute | solution.py:439
  51.8 0.1 collective-permute-start.6
  51.9 22.9 %all-to-all-done.1.ca_ref = bf16[16,8,8,1024]{3,2,1,0:T(8,128)(2,1)S(1)} async-done(((bf16[16,8,8,1024]{3,2,1,0:T(8,128)(2,1)}), bf16[16,8,8,1024]{3,2,1,0:T(8,128)(2,1)S(1)}, u32[]{:S(2)}, u32[]{:S(2)}) %all-to-all-start.1) | async-done | bytes 2097184 | tf_op jit(solution)/shard_map/all_to_all | solution.py:437
  74.8 0.0 collective-permute-done.3.rest_4_
  74.8 0.0 collective-permute-done.4.rest_5_
  74.8 0.0 collective-permute-done.5.rest_6_
  74.8 2.6 %cross.3 = bf16[16,8,8,1024]{3,2,1,0:T(8,128)(2,1)S(1)} custom-call(s32[2,128]{1,0:T(2,128)S(1)} %get-tuple-element.40.slot_ref, bf16[12,8,1024]{2,1,0:T(8,128)(2,1)S(1)} %copy-done.5, bf16[12,8,1024]{2,1,0:T(8,128)(2,1)S(1)} %collective-permute-done.rest_1_, bf16[12,8,1024]{2,1,0:T(8,128)(2,1)S(1)} %collective-permute-done.1.rest_2_, ...), custom_call_target="tpu_custom_call" | custom-call | tf_op jit(solution)/shard_map/cross/pallas_call | solution.py:282
  77.5 0.0 copy-start.2
  77.5 31.5 %all_to_all.20.cb_ref = bf16[16,8,8,1024]{3,2,1,0:T(8,128)(2,1)S(1)} all-to-all(bf16[16,8,8,1024]{3,2,1,0:T(8,128)(2,1)S(1)} %cross.3), channel_id=1, replica_groups=mesh['pair'=8,'tm'=16] {'tm'}, dimensions={0} | all-to-all | bytes 4194304 | tf_op jit(solution)/shard_map/all_to_all | solution.py:443
  109.0 10.0 %stack.1 = f32[16,8,1024]{2,1,0:T(8,128)S(1)} custom-call(bf16[16,8,8,1024]{3,2,1,0:T(8,128)(2,1)S(1)} %all-to-all-done.1.ca_ref, bf16[16,8,8,1024]{3,2,1,0:T(8,128)(2,1)S(1)} %all_to_all.20.cb_ref, bf16[1024,48]{1,0:T(8,128)(2,1)S(1)} %get-tuple-element.49.s3_ref, bf16[2,512,512]{2,1,0:T(8,128)(2,1)S(1)} %copy-done.2), custom_call_target="tpu_custom_call" | custom-call | tf_op jit(solution)/shard_map/stack/pallas_call | solution.py:362
  119.0 13.4 %all_to_all.21 = f32[16,8,1024]{2,1,0:T(8,128)S(1)} all-to-all(f32[16,8,1024]{2,1,0:T(8,128)S(1)} %stack.1), channel_id=1, replica_groups=mesh['pair'=8,'tm'=16] {'tm'}, dimensions={0} | all-to-all | bytes 1048576 | tf_op jit(solution)/shard_map/all_to_all | solution.py:445
  132.4 2.9 %lags.1 = f32[128,2048]{1,0:T(8,128)} custom-call(f32[128,1024]{1,0:T(8,128)S(1)} %bitcast.12, bf16[1024,2048]{1,0:T(8,128)(2,1)S(1)} %copy-done.1), custom_call_target="tpu_custom_call" | custom-call | tf_op jit(solution)/shard_map/lags/pallas_call | solution.py:392
  (14 shorter events, 0.0 us)
Async XLA Ops:
  6.6 27.0 %all-to-all-start = ((bf16[8,12,8,1024]{3,2,1,0:T(8,128)(2,1)}), bf16[8,12,8,1024]{3,2,1,0:T(8,128)(2,1)S(1)}, u32[]{:S(2)}, u32[]{:S(2)}) async-start(bf16[8,12,8,1024]{3,2,1,0:T(8,128)(2,1)} %bitcast.13), calls=%async_computation | async-start | bytes 3145728 | tf_op jit(solution)/shard_map/all_to_all | solution.py:421
  12.0 6.7 %copy-start.3 = (f32[2,32,2048]{2,1,0:T(8,128)S(1)}, f32[2,32,2048]{2,1,0:T(8,128)}, u32[]{:S(2)}) copy-start(f32[2,32,2048]{2,1,0:T(8,128)} %constant.42.clone.base_ref) | copy-start | bytes 1572868
  12.0 6.7 %copy-start.4 = (f32[2,16,2048]{2,1,0:T(8,128)S(1)}, f32[2,16,2048]{2,1,0:T(8,128)}, u32[]{:S(2)}) copy-start(f32[2,16,2048]{2,1,0:T(8,128)} %constant.43.clone.step_ref) | copy-start | bytes 786436
  12.1 6.7 %copy-start.6 = (f32[16,2048]{1,0:T(8,128)S(1)}, f32[16,2048]{1,0:T(8,128)}, u32[]{:S(2)}) copy-start(f32[16,2048]{1,0:T(8,128)} %sketch_ref.1) | copy-start | bytes 393220
  21.9 2.0 %copy-start = (bf16[1024,2048]{1,0:T(8,128)(2,1)}, bf16[1024,2048]{1,0:T(8,128)(2,1)S(1)}, u32[]{:S(2)}) copy-start(bf16[1024,2048]{1,0:T(8,128)(2,1)S(1)} %get-tuple-element.50.inv_ref) | copy-start | bytes 12582916
  36.5 38.3 %copy-start.5 = (bf16[12,8,1024]{2,1,0:T(8,128)(2,1)S(1)}, bf16[12,8,1024]{2,1,0:T(8,128)(2,1)}, u32[]{:S(2)}) copy-start(bf16[12,8,1024]{2,1,0:T(8,128)(2,1)} %get-tuple-element.41.rest_0_) | copy-start | bytes 589828
  36.5 38.3 %all-to-all-start.1 = ((bf16[16,8,8,1024]{3,2,1,0:T(8,128)(2,1)}), bf16[16,8,8,1024]{3,2,1,0:T(8,128)(2,1)S(1)}, u32[]{:S(2)}, u32[]{:S(2)}) async-start(bf16[16,8,8,1024]{3,2,1,0:T(8,128)(2,1)} %cross.2), calls=%async_computation.1 | async-start | bytes 4194304 | tf_op jit(solution)/shard_map/all_to_all | solution.py:437
  43.7 5.2 %collective-permute-start = (bf16[12,8,1024]{2,1,0:T(8,128)(2,1)}, bf16[12,8,1024]{2,1,0:T(8,128)(2,1)S(1)}, u32[]{:S(2)}, u32[]{:S(2)}) collective-permute-start(bf16[12,8,1024]{2,1,0:T(8,128)(2,1)} %get-tuple-element.42), channel_id=1, source_target_pairs={{0,16},{16,0},{32,48},{48,32},{64,80},{80,64},{96,112},{112,96},{1... | collective-permute-start | bytes 589832 | tf_op jit(solution)/shard_map/ppermute | solution.py:439
  43.8 8.0 %collective-permute-start.1 = (bf16[12,8,1024]{2,1,0:T(8,128)(2,1)}, bf16[12,8,1024]{2,1,0:T(8,128)(2,1)S(1)}, u32[]{:S(2)}, u32[]{:S(2)}) collective-permute-start(bf16[12,8,1024]{2,1,0:T(8,128)(2,1)} %get-tuple-element.43), channel_id=1, source_target_pairs={{0,32},{16,48},{32,0},{48,16},{64,96},{80,112},{96,64},{112,80},{1... | collective-permute-start | bytes 589832 | tf_op jit(solution)/shard_map/ppermute | solution.py:439
  44.4 30.4 %collective-permute-start.2 = (bf16[12,8,1024]{2,1,0:T(8,128)(2,1)}, bf16[12,8,1024]{2,1,0:T(8,128)(2,1)S(1)}, u32[]{:S(2)}, u32[]{:S(2)}) collective-permute-start(bf16[12,8,1024]{2,1,0:T(8,128)(2,1)} %get-tuple-element.44), channel_id=1, source_target_pairs={{0,48},{16,32},{32,16},{48,0},{64,112},{80,96},{96,80},{112,64},{1... | collective-permute-start | bytes 589832 | tf_op jit(solution)/shard_map/ppermute | solution.py:439
  45.6 29.2 %collective-permute-start.3 = (bf16[12,8,1024]{2,1,0:T(8,128)(2,1)}, bf16[12,8,1024]{2,1,0:T(8,128)(2,1)S(1)}, u32[]{:S(2)}, u32[]{:S(2)}) collective-permute-start(bf16[12,8,1024]{2,1,0:T(8,128)(2,1)} %get-tuple-element.45), channel_id=1, source_target_pairs={{0,64},{16,80},{32,96},{48,112},{64,0},{80,16},{96,32},{112,48},{1... | collective-permute-start | bytes 589832 | tf_op jit(solution)/shard_map/ppermute | solution.py:439
  46.5 28.3 %collective-permute-start.4 = (bf16[12,8,1024]{2,1,0:T(8,128)(2,1)}, bf16[12,8,1024]{2,1,0:T(8,128)(2,1)S(1)}, u32[]{:S(2)}, u32[]{:S(2)}) collective-permute-start(bf16[12,8,1024]{2,1,0:T(8,128)(2,1)} %get-tuple-element.46), channel_id=1, source_target_pairs={{0,80},{16,64},{32,112},{48,96},{64,16},{80,0},{96,48},{112,32},{1... | collective-permute-start | bytes 589832 | tf_op jit(solution)/shard_map/ppermute | solution.py:439
  48.8 26.0 %collective-permute-start.5 = (bf16[12,8,1024]{2,1,0:T(8,128)(2,1)}, bf16[12,8,1024]{2,1,0:T(8,128)(2,1)}, u32[]{:S(2)}, u32[]{:S(2)}) collective-permute-start(bf16[12,8,1024]{2,1,0:T(8,128)(2,1)} %get-tuple-element.47), channel_id=1, source_target_pairs={{0,96},{16,112},{32,64},{48,80},{64,32},{80,48},{96,0},{112,16},{1... | collective-permute-start | bytes 589832 | tf_op jit(solution)/shard_map/ppermute | solution.py:439
  51.8 23.1 %collective-permute-start.6 = (bf16[12,8,1024]{2,1,0:T(8,128)(2,1)}, bf16[12,8,1024]{2,1,0:T(8,128)(2,1)}, u32[]{:S(2)}, u32[]{:S(2)}) collective-permute-start(bf16[12,8,1024]{2,1,0:T(8,128)(2,1)} %get-tuple-element.48), channel_id=1, source_target_pairs={{0,112},{16,96},{32,80},{48,64},{64,48},{80,32},{96,16},{112,0},{1... | collective-permute-start | bytes 589832 | tf_op jit(solution)/shard_map/ppermute | solution.py:439
  77.5 31.5 %copy-start.2 = (bf16[2,512,512]{2,1,0:T(8,128)(2,1)S(1)}, bf16[2,512,512]{2,1,0:T(8,128)(2,1)}, u32[]{:S(2)}) copy-start(bf16[2,512,512]{2,1,0:T(8,128)(2,1)} %constant.44.clone.e_ref) | copy-start | bytes 3145732
  109.0 23.4 %copy-start.1 = (bf16[1024,2048]{1,0:T(8,128)(2,1)S(1)}, bf16[1024,2048]{1,0:T(8,128)(2,1)}, u32[]{:S(2)}) copy-start(bf16[1024,2048]{1,0:T(8,128)(2,1)} %copy-done) | copy-start | bytes 12582916

commit v4 on v3

--- a/solution.py
+++ b/solution.py
@@ -78,10 +78,8 @@
     return x[:n] + x[n : 2 * n] + x[2 * n :]
 
 
-def dot_nt(a, b, precision=None):
-    return lax.dot_general(
-        a, b, (((1,), (1,)), ((), ())), preferred_element_type=F32, precision=precision
-    )
+def dot_nt(a, b):
+    return lax.dot_general(a, b, (((1,), (1,)), ((), ())), preferred_element_type=F32)
 
 
 def dot_nn(a, b):
@@ -308,9 +306,9 @@
     probes = []
     for p in range(group):
         c = jnp.concatenate([gather_pair(ca_ref, p), gather_pair(cb_ref, p)], axis=0)
-        probe = sum3(dot_nn(c, s3).T)
+        probe = split3(sum3(dot_nn(c, s3).T))
         probes.append(probe)
-        r_s[:, p, :] = sum3(dot_nn(split3(probe), c))
+        r_s[:, p, :] = sum3(dot_nn(probe, c))
         cf = c.astype(F32)
         en_s[pl.ds(p, 1), :] = jnp.sum(cf * cf, axis=0, keepdims=True)
     raw = r_s[...].reshape(RANK * group, width)
@@ -327,7 +325,8 @@
     for p in range(group):
         c = jnp.concatenate([gather_pair(ca_ref, p), gather_pair(cb_ref, p)], axis=0)
         y = sum3(dot_nt(split3(h_s[:, p, :]), c))
-        gram = dot_nt(y, probes[p], lax.Precision.HIGHEST)
+        gram = sum3(dot_nt(split3(y), probes[p]))
+        gram = gram[:, :RANK] + gram[:, RANK : 2 * RANK] + gram[:, 2 * RANK :]
         y_s[:, p, :] = y
         g_s[:, p, :] = unit
         g_s[:, p, :RANK] = gram
@@ -354,14 +353,14 @@
     for r in range(RANK):
         stack = stack + mix[:, RANK + r : RANK + r + 1] * r_s[r]
     for t in range(parts):
-        o_ref[t] = stack
+        o_ref[t] = stack.astype(BF16)
 
 
 def stack_up(crosses, s3, excess):
     parts, group, windows, width = crosses[0].shape
     return pl.pallas_call(
         stack_kernel,
-        out_shape=jax.ShapeDtypeStruct((parts, group, width), F32),
+        out_shape=jax.ShapeDtypeStruct((parts, group, width), BF16),
         scratch_shapes=[
             pltpu.VMEM((RANK, group, width), F32),
             pltpu.VMEM((RANK, group, width), F32),
@@ -374,16 +373,10 @@
     )(*crosses, s3, excess)
 
 
-def lags_kernel(x_ref, inv_ref, o_ref, x2):
-    rows, block = o_ref.shape
-    i = pl.program_id(0)
-
-    @pl.when(i == 0)
-    def _():
-        x2[...] = split2(x_ref[...])
-
-    y = dot_nn(x2[...], inv_ref[:, pl.ds(pl.multiple_of(i * block, block), block)])
-    o_ref[...] = y[:rows] + y[rows:]
+def lags_kernel(x_ref, inv_ref, o_ref):
+    block = o_ref.shape[1]
+    at = pl.multiple_of(pl.program_id(0) * block, block)
+    o_ref[...] = dot_nn(x_ref[...], inv_ref[:, pl.ds(at, block)])
 
 
 def to_lags(x, inverse):
@@ -398,7 +391,6 @@
             pl.BlockSpec((width, LAGS), lambda i: (0, 0)),
         ],
         out_specs=pl.BlockSpec((rows, block), lambda i: (0, i)),
-        scratch_shapes=[pltpu.VMEM((2 * rows, width), BF16)],
         compiler_params=pltpu.CompilerParams(
             dimension_semantics=("arbitrary",), vmem_limit_bytes=12 << 20
         ),

time: 136 us -> 133 us (0.978)
  blocking collectives: 44.9 us -> 43.1 us
    all_to_all x1, blocking collectives: 13.4 us -> 11.6 us  [local(): stack = lax.all_to_all(stack, 'tm', 0, 0, tiled=True)]
where the time goes in v4:
time: 133 us; the launch traced here: 132 us
  blocking collectives  43.1 us (32%)
  Pallas kernels  33.6 us (25%)
  waiting for transfers between devices  32.7 us (25%)
  starting transfers between devices  19 us (14%)
  local copies, waits for them, and re-layouts  2.67 us (2%)
    all_to_all x1, blocking collectives, local(): lax.all_to_all(correlate(slots_rest, blocks_b, n_tm, jax.ShapeDtypeStruct...  31.5 us
    all_to_all x1, waiting for transfers between devices, local(): lax.all_to_all(correlate(slots, [blocks_a], n_tm, pltpu.HBM), 'tm', 0, 0,...  22.9 us
    pallas_call x2, Pallas kernels, whiten(): pl.pallas_call(functools.partial(whiten_kernel, swapped=bool(half)), out_...  13.3 us
    all_to_all x1, blocking collectives, local(): stack = lax.all_to_all(stack, 'tm', 0, 0, tiled=True)  11.6 us
    pallas_call x1, Pallas kernels, stack_up(): pl.pallas_call(stack_kernel, out_shape=jax.ShapeDtypeStruct((parts, group...  9.32 us
    all_to_all x1, waiting for transfers between devices, local(): arrived = lax.all_to_all(sent_a.reshape(shape), 'pair', 0, 0, tiled=True)  7.96 us
    all_to_all x1, starting transfers between devices, local(): lax.all_to_all(correlate(slots, [blocks_a], n_tm, pltpu.HBM), 'tm', 0, 0,...  7.17 us
    ppermute x7, starting transfers between devices, local(): lax.ppermute(sent_b[x], 'pair', [(o, o ^ x) for o in range(n_pair)])  6.42 us
  transfers between devices with their start and end apart: 9, of which 3 were waited for; matrix products, arithmetic and copies ran while one was open for 1% of the time, Pallas kernels for 7%

profile of v4, /device:TPU:0, one launch (start us, length us, event | category | flops | bytes accessed | tf_op | source)
XLA Modules:
  0.0 132.3 jit_solution(8184477236978836874)
XLA Ops:
  0.0 6.6 %whiten.2 = bf16[96,8,1024]{2,1,0:T(8,128)(2,1)} custom-call(s32[1]{0:T(128)} %bitcast.2.owner_ref, s32[2,1024]{1,0:T(2,128)} %bitcast.14, bf16[64,16,2048]{2,1,0:T(8,128)(2,1)} %rec_ref.3, f32[4,32,512]{2,1,0:T(8,128)} %constant.41.clone.parts_ref), custom_call_target="tpu_custom_call" | custom-call | tf_op jit(solution)/shard_map/whiten/pallas_call | solution.py:183
  6.6 5.4 %all-to-all-start = ((bf16[8,12,8,1024]{3,2,1,0:T(8,128)(2,1)}), bf16[8,12,8,1024]{3,2,1,0:T(8,128)(2,1)S(1)}, u32[]{:S(2)}, u32[]{:S(2)}) async-start(bf16[8,12,8,1024]{3,2,1,0:T(8,128)(2,1)} %bitcast.13), calls=%async_computation | async-start | bytes 3145728 | tf_op jit(solution)/shard_map/all_to_all | solution.py:413
  12.0 0.0 copy-start.4
  12.1 0.0 copy-start.6
  12.1 6.7 %whiten.3 = (bf16[12,8,1024]{2,1,0:T(8,128)(2,1)}, bf16[12,8,1024]{2,1,0:T(8,128)(2,1)}, bf16[12,8,1024]{2,1,0:T(8,128)(2,1)}, bf16[12,8,1024]{2,1,0:T(8,128)(2,...) custom-call(s32[1]{0:T(128)} %bitcast.2.owner_ref, ...), custom_call_target="tpu_custom_call" | custom-call | tf_op jit(solution)/shard_map/whiten/pallas_call | solution.py:183
  18.8 3.1 %inverse_table.1 = (bf16[1024,2048]{1,0:T(8,128)(2,1)S(1)}, bf16[1024,48]{1,0:T(8,128)(2,1)S(1)}) custom-call(f32[16,2048]{1,0:T(8,128)S(1)} %copy-done.6, f32[2,32,2048]{2,1,0:T(8,128)S(1)} %copy-done.3, f32[2,16,2048]{2,1,0:T(8,128)S(1)} %copy-done.4), custom_call_target="tpu_custom_call" | custom-call | tf_op jit(solution)/shard_map/inverse_table/pallas_call | solution.py:232
  21.9 2.0 %copy-done = bf16[1024,2048]{1,0:T(8,128)(2,1)} copy-done((bf16[1024,2048]{1,0:T(8,128)(2,1)}, bf16[1024,2048]{1,0:T(8,128)(2,1)S(1)}, u32[]{:S(2)}) %copy-start) | copy-done | bytes 4194328
  23.9 0.7 dynamic-slice_bitcast_fusion
  24.5 0.7 broadcast_multiply_fusion
  25.2 0.1 fusion
  25.4 0.3 convert_reduce_fusion
  25.7 8.0 %all-to-all-done = bf16[8,12,8,1024]{3,2,1,0:T(8,128)(2,1)S(1)} async-done(((bf16[8,12,8,1024]{3,2,1,0:T(8,128)(2,1)}), bf16[8,12,8,1024]{3,2,1,0:T(8,128)(2,1)S(1)}, u32[]{:S(2)}, u32[]{:S(2)}) %all-to-all-start) | async-done | bytes 1572896 | tf_op jit(solution)/shard_map/all_to_all | solution.py:413
  33.6 2.9 %cross.2 = bf16[16,8,8,1024]{3,2,1,0:T(8,128)(2,1)} custom-call(s32[2,128]{1,0:T(2,128)S(1)} %get-tuple-element.54.slot_ref, bf16[96,8,1024]{2,1,0:T(8,128)(2,1)S(1)} %bitcast.11), custom_call_target="tpu_custom_call" | custom-call | tf_op jit(solution)/shard_map/cross/pallas_call | solution.py:280
  36.5 7.2 %all-to-all-start.1 = ((bf16[16,8,8,1024]{3,2,1,0:T(8,128)(2,1)}), bf16[16,8,8,1024]{3,2,1,0:T(8,128)(2,1)S(1)}, u32[]{:S(2)}, u32[]{:S(2)}) async-start(bf16[16,8,8,1024]{3,2,1,0:T(8,128)(2,1)} %cross.2), calls=%async_computation.1 | async-start | bytes 4194304 | tf_op jit(solution)/shard_map/all_to_all | solution.py:429
  43.7 0.1 collective-permute-start
  43.8 0.6 collective-permute-start.1
  44.4 1.2 collective-permute-start.2
  45.6 0.9 collective-permute-start.3
  46.5 2.3 %collective-permute-start.4 = (bf16[12,8,1024]{2,1,0:T(8,128)(2,1)}, bf16[12,8,1024]{2,1,0:T(8,128)(2,1)S(1)}, u32[]{:S(2)}, u32[]{:S(2)}) collective-permute-start(bf16[12,8,1024]{2,1,0:T(8,128)(2,1)} %get-tuple-element.46), channel_id=1, source_target_pairs={{0,80},{16,64},{32,112},{48,96},{64,16},{80,0},{96,48},{112,32},{1... | collective-permute-start | bytes 589832 | tf_op jit(solution)/shard_map/ppermute | solution.py:431
  48.8 1.2 collective-permute-start.5
  50.0 1.8 %collective-permute-done.1.rest_2_ = bf16[12,8,1024]{2,1,0:T(8,128)(2,1)S(1)} collective-permute-done((bf16[12,8,1024]{2,1,0:T(8,128)(2,1)}, bf16[12,8,1024]{2,1,0:T(8,128)(2,1)S(1)}, u32[]{:S(2)}, u32[]{:S(2)}) %collective-permute-start.1) | collective-permute-done | bytes 196640 | tf_op jit(solution)/shard_map/ppermute | solution.py:431
  51.8 0.1 collective-permute-start.6
  51.9 22.9 %all-to-all-done.1.ca_ref = bf16[16,8,8,1024]{3,2,1,0:T(8,128)(2,1)S(1)} async-done(((bf16[16,8,8,1024]{3,2,1,0:T(8,128)(2,1)}), bf16[16,8,8,1024]{3,2,1,0:T(8,128)(2,1)S(1)}, u32[]{:S(2)}, u32[]{:S(2)}) %all-to-all-start.1) | async-done | bytes 2097184 | tf_op jit(solution)/shard_map/all_to_all | solution.py:429
  74.8 0.0 collective-permute-done.3.rest_4_
  74.8 0.0 collective-permute-done.4.rest_5_
  74.8 0.0 collective-permute-done.5.rest_6_
  74.8 2.6 %cross.3 = bf16[16,8,8,1024]{3,2,1,0:T(8,128)(2,1)S(1)} custom-call(s32[2,128]{1,0:T(2,128)S(1)} %get-tuple-element.40.slot_ref, bf16[12,8,1024]{2,1,0:T(8,128)(2,1)S(1)} %copy-done.5, bf16[12,8,1024]{2,1,0:T(8,128)(2,1)S(1)} %collective-permute-done.rest_1_, bf16[12,8,1024]{2,1,0:T(8,128)(2,1)S(1)} %collective-permute-done.1.rest_2_, ...), custom_call_target="tpu_custom_call" | custom-call | tf_op jit(solution)/shard_map/cross/pallas_call | solution.py:280
  77.5 0.0 copy-start.2
  77.5 31.5 %all_to_all.20.cb_ref = bf16[16,8,8,1024]{3,2,1,0:T(8,128)(2,1)S(1)} all-to-all(bf16[16,8,8,1024]{3,2,1,0:T(8,128)(2,1)S(1)} %cross.3), channel_id=1, replica_groups=mesh['pair'=8,'tm'=16] {'tm'}, dimensions={0} | all-to-all | bytes 4194304 | tf_op jit(solution)/shard_map/all_to_all | solution.py:435
  109.0 9.3 %stack.1 = bf16[16,8,1024]{2,1,0:T(8,128)(2,1)S(1)} custom-call(bf16[16,8,8,1024]{3,2,1,0:T(8,128)(2,1)S(1)} %all-to-all-done.1.ca_ref, bf16[16,8,8,1024]{3,2,1,0:T(8,128)(2,1)S(1)} %all_to_all.20.cb_ref, bf16[1024,48]{1,0:T(8,128)(2,1)S(1)} %get-tuple-element.49.s3_ref, bf16[2,512,512]{2,1,0:T(8,128)(2,1)S(1)} %copy-done.2), custom_call_target="tpu_custom_call" | custom-call | tf_op jit(solution)/shard_map/stack/pallas_call | solution.py:361
  118.3 11.6 %all_to_all.21 = bf16[16,8,1024]{2,1,0:T(8,128)(2,1)S(1)} all-to-all(bf16[16,8,1024]{2,1,0:T(8,128)(2,1)S(1)} %stack.1), channel_id=1, replica_groups=mesh['pair'=8,'tm'=16] {'tm'}, dimensions={0} | all-to-all | bytes 524288 | tf_op jit(solution)/shard_map/all_to_all | solution.py:437
  129.9 2.4 %lags.1 = f32[128,2048]{1,0:T(8,128)} custom-call(bf16[128,1024]{1,0:T(8,128)(2,1)S(1)} %bitcast.12, bf16[1024,2048]{1,0:T(8,128)(2,1)S(1)} %copy-done.1), custom_call_target="tpu_custom_call" | custom-call | tf_op jit(solution)/shard_map/lags/pallas_call | solution.py:385
  (14 shorter events, 0.0 us)
Async XLA Ops:
  6.6 27.0 %all-to-all-start = ((bf16[8,12,8,1024]{3,2,1,0:T(8,128)(2,1)}), bf16[8,12,8,1024]{3,2,1,0:T(8,128)(2,1)S(1)}, u32[]{:S(2)}, u32[]{:S(2)}) async-start(bf16[8,12,8,1024]{3,2,1,0:T(8,128)(2,1)} %bitcast.13), calls=%async_computation | async-start | bytes 3145728 | tf_op jit(solution)/shard_map/all_to_all | solution.py:413
  12.0 6.7 %copy-start.3 = (f32[2,32,2048]{2,1,0:T(8,128)S(1)}, f32[2,32,2048]{2,1,0:T(8,128)}, u32[]{:S(2)}) copy-start(f32[2,32,2048]{2,1,0:T(8,128)} %constant.42.clone.base_ref) | copy-start | bytes 1572868
  12.0 6.7 %copy-start.4 = (f32[2,16,2048]{2,1,0:T(8,128)S(1)}, f32[2,16,2048]{2,1,0:T(8,128)}, u32[]{:S(2)}) copy-start(f32[2,16,2048]{2,1,0:T(8,128)} %constant.43.clone.step_ref) | copy-start | bytes 786436
  12.1 6.7 %copy-start.6 = (f32[16,2048]{1,0:T(8,128)S(1)}, f32[16,2048]{1,0:T(8,128)}, u32[]{:S(2)}) copy-start(f32[16,2048]{1,0:T(8,128)} %sketch_ref.1) | copy-start | bytes 393220
  21.9 2.0 %copy-start = (bf16[1024,2048]{1,0:T(8,128)(2,1)}, bf16[1024,2048]{1,0:T(8,128)(2,1)S(1)}, u32[]{:S(2)}) copy-start(bf16[1024,2048]{1,0:T(8,128)(2,1)S(1)} %get-tuple-element.50.inv_ref) | copy-start | bytes 12582916
  36.5 38.3 %copy-start.5 = (bf16[12,8,1024]{2,1,0:T(8,128)(2,1)S(1)}, bf16[12,8,1024]{2,1,0:T(8,128)(2,1)}, u32[]{:S(2)}) copy-start(bf16[12,8,1024]{2,1,0:T(8,128)(2,1)} %get-tuple-element.41.rest_0_) | copy-start | bytes 589828
  36.5 38.3 %all-to-all-start.1 = ((bf16[16,8,8,1024]{3,2,1,0:T(8,128)(2,1)}), bf16[16,8,8,1024]{3,2,1,0:T(8,128)(2,1)S(1)}, u32[]{:S(2)}, u32[]{:S(2)}) async-start(bf16[16,8,8,1024]{3,2,1,0:T(8,128)(2,1)} %cross.2), calls=%async_computation.1 | async-start | bytes 4194304 | tf_op jit(solution)/shard_map/all_to_all | solution.py:429
  43.7 5.2 %collective-permute-start = (bf16[12,8,1024]{2,1,0:T(8,128)(2,1)}, bf16[12,8,1024]{2,1,0:T(8,128)(2,1)S(1)}, u32[]{:S(2)}, u32[]{:S(2)}) collective-permute-start(bf16[12,8,1024]{2,1,0:T(8,128)(2,1)} %get-tuple-element.42), channel_id=1, source_target_pairs={{0,16},{16,0},{32,48},{48,32},{64,80},{80,64},{96,112},{112,96},{1... | collective-permute-start | bytes 589832 | tf_op jit(solution)/shard_map/ppermute | solution.py:431
  43.8 8.0 %collective-permute-start.1 = (bf16[12,8,1024]{2,1,0:T(8,128)(2,1)}, bf16[12,8,1024]{2,1,0:T(8,128)(2,1)S(1)}, u32[]{:S(2)}, u32[]{:S(2)}) collective-permute-start(bf16[12,8,1024]{2,1,0:T(8,128)(2,1)} %get-tuple-element.43), channel_id=1, source_target_pairs={{0,32},{16,48},{32,0},{48,16},{64,96},{80,112},{96,64},{112,80},{1... | collective-permute-start | bytes 589832 | tf_op jit(solution)/shard_map/ppermute | solution.py:431
  44.4 30.4 %collective-permute-start.2 = (bf16[12,8,1024]{2,1,0:T(8,128)(2,1)}, bf16[12,8,1024]{2,1,0:T(8,128)(2,1)S(1)}, u32[]{:S(2)}, u32[]{:S(2)}) collective-permute-start(bf16[12,8,1024]{2,1,0:T(8,128)(2,1)} %get-tuple-element.44), channel_id=1, source_target_pairs={{0,48},{16,32},{32,16},{48,0},{64,112},{80,96},{96,80},{112,64},{1... | collective-permute-start | bytes 589832 | tf_op jit(solution)/shard_map/ppermute | solution.py:431
  45.6 29.2 %collective-permute-start.3 = (bf16[12,8,1024]{2,1,0:T(8,128)(2,1)}, bf16[12,8,1024]{2,1,0:T(8,128)(2,1)S(1)}, u32[]{:S(2)}, u32[]{:S(2)}) collective-permute-start(bf16[12,8,1024]{2,1,0:T(8,128)(2,1)} %get-tuple-element.45), channel_id=1, source_target_pairs={{0,64},{16,80},{32,96},{48,112},{64,0},{80,16},{96,32},{112,48},{1... | collective-permute-start | bytes 589832 | tf_op jit(solution)/shard_map/ppermute | solution.py:431
  46.5 28.3 %collective-permute-start.4 = (bf16[12,8,1024]{2,1,0:T(8,128)(2,1)}, bf16[12,8,1024]{2,1,0:T(8,128)(2,1)S(1)}, u32[]{:S(2)}, u32[]{:S(2)}) collective-permute-start(bf16[12,8,1024]{2,1,0:T(8,128)(2,1)} %get-tuple-element.46), channel_id=1, source_target_pairs={{0,80},{16,64},{32,112},{48,96},{64,16},{80,0},{96,48},{112,32},{1... | collective-permute-start | bytes 589832 | tf_op jit(solution)/shard_map/ppermute | solution.py:431
  48.8 26.0 %collective-permute-start.5 = (bf16[12,8,1024]{2,1,0:T(8,128)(2,1)}, bf16[12,8,1024]{2,1,0:T(8,128)(2,1)}, u32[]{:S(2)}, u32[]{:S(2)}) collective-permute-start(bf16[12,8,1024]{2,1,0:T(8,128)(2,1)} %get-tuple-element.47), channel_id=1, source_target_pairs={{0,96},{16,112},{32,64},{48,80},{64,32},{80,48},{96,0},{112,16},{1... | collective-permute-start | bytes 589832 | tf_op jit(solution)/shard_map/ppermute | solution.py:431
  51.8 23.1 %collective-permute-start.6 = (bf16[12,8,1024]{2,1,0:T(8,128)(2,1)}, bf16[12,8,1024]{2,1,0:T(8,128)(2,1)}, u32[]{:S(2)}, u32[]{:S(2)}) collective-permute-start(bf16[12,8,1024]{2,1,0:T(8,128)(2,1)} %get-tuple-element.48), channel_id=1, source_target_pairs={{0,112},{16,96},{32,80},{48,64},{64,48},{80,32},{96,16},{112,0},{1... | collective-permute-start | bytes 589832 | tf_op jit(solution)/shard_map/ppermute | solution.py:431
  77.5 31.5 %copy-start.2 = (bf16[2,512,512]{2,1,0:T(8,128)(2,1)S(1)}, bf16[2,512,512]{2,1,0:T(8,128)(2,1)}, u32[]{:S(2)}) copy-start(bf16[2,512,512]{2,1,0:T(8,128)(2,1)} %constant.44.clone.e_ref) | copy-start | bytes 3145732
  109.0 21.0 %copy-start.1 = (bf16[1024,2048]{1,0:T(8,128)(2,1)S(1)}, bf16[1024,2048]{1,0:T(8,128)(2,1)}, u32[]{:S(2)}) copy-start(bf16[1024,2048]{1,0:T(8,128)(2,1)} %copy-done) | copy-start | bytes 12582916

commit v5 on v4

--- a/solution.py
+++ b/solution.py
@@ -381,7 +381,7 @@
 
 def to_lags(x, inverse):
     rows, width = x.shape
-    block = 512
+    block = 1024
     return pl.pallas_call(
         lags_kernel,
         out_shape=jax.ShapeDtypeStruct((rows, LAGS), F32),

time: 133 us -> 132 us (level)
  no operation moved by 1% of the time
where the time goes in v5:
time: 132 us
  blocking collectives  43.1 us (33%)
  Pallas kernels  33 us (25%)
  waiting for transfers between devices  32.7 us (25%)
  starting transfers between devices  19 us (14%)
  local copies, waits for them, and re-layouts  2.67 us (2%)
    all_to_all x1, blocking collectives, local(): lax.all_to_all(correlate(slots_rest, blocks_b, n_tm, jax.ShapeDtypeStruct...  31.5 us
    all_to_all x1, waiting for transfers between devices, local(): lax.all_to_all(correlate(slots, [blocks_a], n_tm, pltpu.HBM), 'tm', 0, 0,...  22.9 us
    pallas_call x2, Pallas kernels, whiten(): pl.pallas_call(functools.partial(whiten_kernel, swapped=bool(half)), out_...  13.3 us
    all_to_all x1, blocking collectives, local(): stack = lax.all_to_all(stack, 'tm', 0, 0, tiled=True)  11.6 us
    pallas_call x1, Pallas kernels, stack_up(): pl.pallas_call(stack_kernel, out_shape=jax.ShapeDtypeStruct((parts, group...  9.32 us
    all_to_all x1, waiting for transfers between devices, local(): arrived = lax.all_to_all(sent_a.reshape(shape), 'pair', 0, 0, tiled=True)  7.96 us
    all_to_all x1, starting transfers between devices, local(): lax.all_to_all(correlate(slots, [blocks_a], n_tm, pltpu.HBM), 'tm', 0, 0,...  7.17 us
    ppermute x7, starting transfers between devices, local(): lax.ppermute(sent_b[x], 'pair', [(o, o ^ x) for o in range(n_pair)])  6.42 us
  transfers between devices with their start and end apart: 9, of which 3 were waited for; matrix products, arithmetic and copies ran while one was open for 1% of the time, Pallas kernels for 7%

profile of v5, /device:TPU:0, one launch (start us, length us, event | category | flops | bytes accessed | tf_op | source)
XLA Modules:
  0.0 131.7 jit_solution(12613988736931686648)
XLA Ops:
  0.0 6.6 %whiten.2 = bf16[96,8,1024]{2,1,0:T(8,128)(2,1)} custom-call(s32[1]{0:T(128)} %bitcast.2.owner_ref, s32[2,1024]{1,0:T(2,128)} %bitcast.14, bf16[64,16,2048]{2,1,0:T(8,128)(2,1)} %rec_ref.3, f32[4,32,512]{2,1,0:T(8,128)} %constant.41.clone.parts_ref), custom_call_target="tpu_custom_call" | custom-call | tf_op jit(solution)/shard_map/whiten/pallas_call | solution.py:183
  6.6 5.4 %all-to-all-start = ((bf16[8,12,8,1024]{3,2,1,0:T(8,128)(2,1)}), bf16[8,12,8,1024]{3,2,1,0:T(8,128)(2,1)S(1)}, u32[]{:S(2)}, u32[]{:S(2)}) async-start(bf16[8,12,8,1024]{3,2,1,0:T(8,128)(2,1)} %bitcast.13), calls=%async_computation | async-start | bytes 3145728 | tf_op jit(solution)/shard_map/all_to_all | solution.py:413
  12.0 0.0 copy-start.4
  12.1 0.0 copy-start.6
  12.1 6.7 %whiten.3 = (bf16[12,8,1024]{2,1,0:T(8,128)(2,1)}, bf16[12,8,1024]{2,1,0:T(8,128)(2,1)}, bf16[12,8,1024]{2,1,0:T(8,128)(2,1)}, bf16[12,8,1024]{2,1,0:T(8,128)(2,...) custom-call(s32[1]{0:T(128)} %bitcast.2.owner_ref, ...), custom_call_target="tpu_custom_call" | custom-call | tf_op jit(solution)/shard_map/whiten/pallas_call | solution.py:183
  18.8 3.1 %inverse_table.1 = (bf16[1024,2048]{1,0:T(8,128)(2,1)S(1)}, bf16[1024,48]{1,0:T(8,128)(2,1)S(1)}) custom-call(f32[16,2048]{1,0:T(8,128)S(1)} %copy-done.6, f32[2,32,2048]{2,1,0:T(8,128)S(1)} %copy-done.3, f32[2,16,2048]{2,1,0:T(8,128)S(1)} %copy-done.4), custom_call_target="tpu_custom_call" | custom-call | tf_op jit(solution)/shard_map/inverse_table/pallas_call | solution.py:232
  21.9 2.0 %copy-done = bf16[1024,2048]{1,0:T(8,128)(2,1)} copy-done((bf16[1024,2048]{1,0:T(8,128)(2,1)}, bf16[1024,2048]{1,0:T(8,128)(2,1)S(1)}, u32[]{:S(2)}) %copy-start) | copy-done | bytes 4194328
  23.9 0.7 dynamic-slice_bitcast_fusion
  24.5 0.7 broadcast_multiply_fusion
  25.2 0.1 fusion
  25.4 0.3 convert_reduce_fusion
  25.7 8.0 %all-to-all-done = bf16[8,12,8,1024]{3,2,1,0:T(8,128)(2,1)S(1)} async-done(((bf16[8,12,8,1024]{3,2,1,0:T(8,128)(2,1)}), bf16[8,12,8,1024]{3,2,1,0:T(8,128)(2,1)S(1)}, u32[]{:S(2)}, u32[]{:S(2)}) %all-to-all-start) | async-done | bytes 1572896 | tf_op jit(solution)/shard_map/all_to_all | solution.py:413
  33.6 2.9 %cross.2 = bf16[16,8,8,1024]{3,2,1,0:T(8,128)(2,1)} custom-call(s32[2,128]{1,0:T(2,128)S(1)} %get-tuple-element.54.slot_ref, bf16[96,8,1024]{2,1,0:T(8,128)(2,1)S(1)} %bitcast.11), custom_call_target="tpu_custom_call" | custom-call | tf_op jit(solution)/shard_map/cross/pallas_call | solution.py:280
  36.5 7.2 %all-to-all-start.1 = ((bf16[16,8,8,1024]{3,2,1,0:T(8,128)(2,1)}), bf16[16,8,8,1024]{3,2,1,0:T(8,128)(2,1)S(1)}, u32[]{:S(2)}, u32[]{:S(2)}) async-start(bf16[16,8,8,1024]{3,2,1,0:T(8,128)(2,1)} %cross.2), calls=%async_computation.1 | async-start | bytes 4194304 | tf_op jit(solution)/shard_map/all_to_all | solution.py:429
  43.7 0.1 collective-permute-start
  43.8 0.6 collective-permute-start.1
  44.4 1.2 collective-permute-start.2
  45.6 0.9 collective-permute-start.3
  46.5 2.3 %collective-permute-start.4 = (bf16[12,8,1024]{2,1,0:T(8,128)(2,1)}, bf16[12,8,1024]{2,1,0:T(8,128)(2,1)S(1)}, u32[]{:S(2)}, u32[]{:S(2)}) collective-permute-start(bf16[12,8,1024]{2,1,0:T(8,128)(2,1)} %get-tuple-element.46), channel_id=1, source_target_pairs={{0,80},{16,64},{32,112},{48,96},{64,16},{80,0},{96,48},{112,32},{1... | collective-permute-start | bytes 589832 | tf_op jit(solution)/shard_map/ppermute | solution.py:431
  48.8 1.2 collective-permute-start.5
  50.0 1.8 %collective-permute-done.1.rest_2_ = bf16[12,8,1024]{2,1,0:T(8,128)(2,1)S(1)} collective-permute-done((bf16[12,8,1024]{2,1,0:T(8,128)(2,1)}, bf16[12,8,1024]{2,1,0:T(8,128)(2,1)S(1)}, u32[]{:S(2)}, u32[]{:S(2)}) %collective-permute-start.1) | collective-permute-done | bytes 196640 | tf_op jit(solution)/shard_map/ppermute | solution.py:431
  51.8 0.1 collective-permute-start.6
  51.9 22.9 %all-to-all-done.1.ca_ref = bf16[16,8,8,1024]{3,2,1,0:T(8,128)(2,1)S(1)} async-done(((bf16[16,8,8,1024]{3,2,1,0:T(8,128)(2,1)}), bf16[16,8,8,1024]{3,2,1,0:T(8,128)(2,1)S(1)}, u32[]{:S(2)}, u32[]{:S(2)}) %all-to-all-start.1) | async-done | bytes 2097184 | tf_op jit(solution)/shard_map/all_to_all | solution.py:429
  74.8 0.0 collective-permute-done.3.rest_4_
  74.8 0.0 collective-permute-done.4.rest_5_
  74.8 0.0 collective-permute-done.5.rest_6_
  74.8 2.6 %cross.3 = bf16[16,8,8,1024]{3,2,1,0:T(8,128)(2,1)S(1)} custom-call(s32[2,128]{1,0:T(2,128)S(1)} %get-tuple-element.40.slot_ref, bf16[12,8,1024]{2,1,0:T(8,128)(2,1)S(1)} %copy-done.5, bf16[12,8,1024]{2,1,0:T(8,128)(2,1)S(1)} %collective-permute-done.rest_1_, bf16[12,8,1024]{2,1,0:T(8,128)(2,1)S(1)} %collective-permute-done.1.rest_2_, ...), custom_call_target="tpu_custom_call" | custom-call | tf_op jit(solution)/shard_map/cross/pallas_call | solution.py:280
  77.5 0.0 copy-start.2
  77.5 31.5 %all_to_all.20.cb_ref = bf16[16,8,8,1024]{3,2,1,0:T(8,128)(2,1)S(1)} all-to-all(bf16[16,8,8,1024]{3,2,1,0:T(8,128)(2,1)S(1)} %cross.3), channel_id=1, replica_groups=mesh['pair'=8,'tm'=16] {'tm'}, dimensions={0} | all-to-all | bytes 4194304 | tf_op jit(solution)/shard_map/all_to_all | solution.py:435
  109.0 9.3 %stack.1 = bf16[16,8,1024]{2,1,0:T(8,128)(2,1)S(1)} custom-call(bf16[16,8,8,1024]{3,2,1,0:T(8,128)(2,1)S(1)} %all-to-all-done.1.ca_ref, bf16[16,8,8,1024]{3,2,1,0:T(8,128)(2,1)S(1)} %all_to_all.20.cb_ref, bf16[1024,48]{1,0:T(8,128)(2,1)S(1)} %get-tuple-element.49.s3_ref, bf16[2,512,512]{2,1,0:T(8,128)(2,1)S(1)} %copy-done.2), custom_call_target="tpu_custom_call" | custom-call | tf_op jit(solution)/shard_map/stack/pallas_call | solution.py:361
  118.3 11.6 %all_to_all.21 = bf16[16,8,1024]{2,1,0:T(8,128)(2,1)S(1)} all-to-all(bf16[16,8,1024]{2,1,0:T(8,128)(2,1)S(1)} %stack.1), channel_id=1, replica_groups=mesh['pair'=8,'tm'=16] {'tm'}, dimensions={0} | all-to-all | bytes 524288 | tf_op jit(solution)/shard_map/all_to_all | solution.py:437
  129.9 1.7 %lags.1 = f32[128,2048]{1,0:T(8,128)} custom-call(bf16[128,1024]{1,0:T(8,128)(2,1)S(1)} %bitcast.12, bf16[1024,2048]{1,0:T(8,128)(2,1)S(1)} %copy-done.1), custom_call_target="tpu_custom_call" | custom-call | tf_op jit(solution)/shard_map/lags/pallas_call | solution.py:385
  (14 shorter events, 0.0 us)
Async XLA Ops:
  6.6 27.0 %all-to-all-start = ((bf16[8,12,8,1024]{3,2,1,0:T(8,128)(2,1)}), bf16[8,12,8,1024]{3,2,1,0:T(8,128)(2,1)S(1)}, u32[]{:S(2)}, u32[]{:S(2)}) async-start(bf16[8,12,8,1024]{3,2,1,0:T(8,128)(2,1)} %bitcast.13), calls=%async_computation | async-start | bytes 3145728 | tf_op jit(solution)/shard_map/all_to_all | solution.py:413
  12.0 6.7 %copy-start.3 = (f32[2,32,2048]{2,1,0:T(8,128)S(1)}, f32[2,32,2048]{2,1,0:T(8,128)}, u32[]{:S(2)}) copy-start(f32[2,32,2048]{2,1,0:T(8,128)} %constant.42.clone.base_ref) | copy-start | bytes 1572868
  12.0 6.7 %copy-start.4 = (f32[2,16,2048]{2,1,0:T(8,128)S(1)}, f32[2,16,2048]{2,1,0:T(8,128)}, u32[]{:S(2)}) copy-start(f32[2,16,2048]{2,1,0:T(8,128)} %constant.43.clone.step_ref) | copy-start | bytes 786436
  12.1 6.7 %copy-start.6 = (f32[16,2048]{1,0:T(8,128)S(1)}, f32[16,2048]{1,0:T(8,128)}, u32[]{:S(2)}) copy-start(f32[16,2048]{1,0:T(8,128)} %sketch_ref.1) | copy-start | bytes 393220
  21.9 2.0 %copy-start = (bf16[1024,2048]{1,0:T(8,128)(2,1)}, bf16[1024,2048]{1,0:T(8,128)(2,1)S(1)}, u32[]{:S(2)}) copy-start(bf16[1024,2048]{1,0:T(8,128)(2,1)S(1)} %get-tuple-element.50.inv_ref) | copy-start | bytes 12582916
  36.5 38.3 %copy-start.5 = (bf16[12,8,1024]{2,1,0:T(8,128)(2,1)S(1)}, bf16[12,8,1024]{2,1,0:T(8,128)(2,1)}, u32[]{:S(2)}) copy-start(bf16[12,8,1024]{2,1,0:T(8,128)(2,1)} %get-tuple-element.41.rest_0_) | copy-start | bytes 589828
  36.5 38.3 %all-to-all-start.1 = ((bf16[16,8,8,1024]{3,2,1,0:T(8,128)(2,1)}), bf16[16,8,8,1024]{3,2,1,0:T(8,128)(2,1)S(1)}, u32[]{:S(2)}, u32[]{:S(2)}) async-start(bf16[16,8,8,1024]{3,2,1,0:T(8,128)(2,1)} %cross.2), calls=%async_computation.1 | async-start | bytes 4194304 | tf_op jit(solution)/shard_map/all_to_all | solution.py:429
  43.7 5.2 %collective-permute-start = (bf16[12,8,1024]{2,1,0:T(8,128)(2,1)}, bf16[12,8,1024]{2,1,0:T(8,128)(2,1)S(1)}, u32[]{:S(2)}, u32[]{:S(2)}) collective-permute-start(bf16[12,8,1024]{2,1,0:T(8,128)(2,1)} %get-tuple-element.42), channel_id=1, source_target_pairs={{0,16},{16,0},{32,48},{48,32},{64,80},{80,64},{96,112},{112,96},{1... | collective-permute-start | bytes 589832 | tf_op jit(solution)/shard_map/ppermute | solution.py:431
  43.8 8.0 %collective-permute-start.1 = (bf16[12,8,1024]{2,1,0:T(8,128)(2,1)}, bf16[12,8,1024]{2,1,0:T(8,128)(2,1)S(1)}, u32[]{:S(2)}, u32[]{:S(2)}) collective-permute-start(bf16[12,8,1024]{2,1,0:T(8,128)(2,1)} %get-tuple-element.43), channel_id=1, source_target_pairs={{0,32},{16,48},{32,0},{48,16},{64,96},{80,112},{96,64},{112,80},{1... | collective-permute-start | bytes 589832 | tf_op jit(solution)/shard_map/ppermute | solution.py:431
  44.4 30.4 %collective-permute-start.2 = (bf16[12,8,1024]{2,1,0:T(8,128)(2,1)}, bf16[12,8,1024]{2,1,0:T(8,128)(2,1)S(1)}, u32[]{:S(2)}, u32[]{:S(2)}) collective-permute-start(bf16[12,8,1024]{2,1,0:T(8,128)(2,1)} %get-tuple-element.44), channel_id=1, source_target_pairs={{0,48},{16,32},{32,16},{48,0},{64,112},{80,96},{96,80},{112,64},{1... | collective-permute-start | bytes 589832 | tf_op jit(solution)/shard_map/ppermute | solution.py:431
  45.6 29.2 %collective-permute-start.3 = (bf16[12,8,1024]{2,1,0:T(8,128)(2,1)}, bf16[12,8,1024]{2,1,0:T(8,128)(2,1)S(1)}, u32[]{:S(2)}, u32[]{:S(2)}) collective-permute-start(bf16[12,8,1024]{2,1,0:T(8,128)(2,1)} %get-tuple-element.45), channel_id=1, source_target_pairs={{0,64},{16,80},{32,96},{48,112},{64,0},{80,16},{96,32},{112,48},{1... | collective-permute-start | bytes 589832 | tf_op jit(solution)/shard_map/ppermute | solution.py:431
  46.5 28.3 %collective-permute-start.4 = (bf16[12,8,1024]{2,1,0:T(8,128)(2,1)}, bf16[12,8,1024]{2,1,0:T(8,128)(2,1)S(1)}, u32[]{:S(2)}, u32[]{:S(2)}) collective-permute-start(bf16[12,8,1024]{2,1,0:T(8,128)(2,1)} %get-tuple-element.46), channel_id=1, source_target_pairs={{0,80},{16,64},{32,112},{48,96},{64,16},{80,0},{96,48},{112,32},{1... | collective-permute-start | bytes 589832 | tf_op jit(solution)/shard_map/ppermute | solution.py:431
  48.8 26.0 %collective-permute-start.5 = (bf16[12,8,1024]{2,1,0:T(8,128)(2,1)}, bf16[12,8,1024]{2,1,0:T(8,128)(2,1)}, u32[]{:S(2)}, u32[]{:S(2)}) collective-permute-start(bf16[12,8,1024]{2,1,0:T(8,128)(2,1)} %get-tuple-element.47), channel_id=1, source_target_pairs={{0,96},{16,112},{32,64},{48,80},{64,32},{80,48},{96,0},{112,16},{1... | collective-permute-start | bytes 589832 | tf_op jit(solution)/shard_map/ppermute | solution.py:431
  51.8 23.1 %collective-permute-start.6 = (bf16[12,8,1024]{2,1,0:T(8,128)(2,1)}, bf16[12,8,1024]{2,1,0:T(8,128)(2,1)}, u32[]{:S(2)}, u32[]{:S(2)}) collective-permute-start(bf16[12,8,1024]{2,1,0:T(8,128)(2,1)} %get-tuple-element.48), channel_id=1, source_target_pairs={{0,112},{16,96},{32,80},{48,64},{64,48},{80,32},{96,16},{112,0},{1... | collective-permute-start | bytes 589832 | tf_op jit(solution)/shard_map/ppermute | solution.py:431
  77.5 31.5 %copy-start.2 = (bf16[2,512,512]{2,1,0:T(8,128)(2,1)S(1)}, bf16[2,512,512]{2,1,0:T(8,128)(2,1)}, u32[]{:S(2)}) copy-start(bf16[2,512,512]{2,1,0:T(8,128)(2,1)} %constant.44.clone.e_ref) | copy-start | bytes 3145732
  109.0 21.0 %copy-start.1 = (bf16[1024,2048]{1,0:T(8,128)(2,1)S(1)}, bf16[1024,2048]{1,0:T(8,128)(2,1)}, u32[]{:S(2)}) copy-start(bf16[1024,2048]{1,0:T(8,128)(2,1)} %copy-done) | copy-start | bytes 12582916
